TPU v7x, 256 devices: a whole 4x4x8 slice. The times are simulated.
256 devices in a mesh: ctx: 32 (over y, x, core), fsdp: 4 (over z_hi), tp: 2 (over z_lo).
Axes of the slice: x: 4, y: 4, z: 8 (z_hi: 4, z_lo: 2; z = z_hi * 2 + z_lo), core: 2. Of those that a mesh axis runs over, the one named last changes fastest.
Arguments:
- query_gate: bfloat16 [4, 4096, 8192], P('fsdp', 'ctx', 'tp'), may hold values from -6 to 6
- key_proj: bfloat16 [4, 4096, 8192], P('fsdp', 'ctx', 'tp'), may hold values from -6 to 6
- value_proj: bfloat16 [4, 4096, 8192], P('fsdp', 'ctx', 'tp'), may hold values from -6 to 6
- grad_out: bfloat16 [4, 4096, 8192], P('fsdp', 'ctx', 'tp'), may hold values from -6 to 6
- filters: float32 [128, 8192], P('fsdp', 'tp'), may hold values from -0.5 to 0.5
- doc_bounds: int32 [4, 49], P('fsdp'), may hold values from 0 to 4032, as said below
- continues: int32 [4, 32], P('fsdp', 'ctx'), may hold values from 0 to 1, as said below
Outputs:
- grad_query: bfloat16 [4, 4096, 8192], P('fsdp', 'ctx', 'tp')
- grad_key: bfloat16 [4, 4096, 8192], P('fsdp', 'ctx', 'tp')
- grad_value: bfloat16 [4, 4096, 8192], P('fsdp', 'ctx', 'tp')
- grad_filter: float32 [128, 8192], P('fsdp', 'tp')
Inputs may be any that keep to these rules, and one draw needn't show every extreme that they name: Each row of doc_bounds increases strictly and begins with 0. continues[w, d] is 0 for d = 0 and wherever a document of window w begins at token d * 128; at other shard edges it may be 0 or 1 (the sequence is cut there or not).
All inputs are finite; a program needn't handle non-finite values.
Results may differ from a plain program's by a relative error of at most 0.0065.
Values may be sent and summed in bfloat16 or wider, within the bound.
A program may use at most 64 MiB of HBM per device.

v0:
```python
import math

import jax
import jax.numpy as jnp
from jax import lax
from jax.sharding import PartitionSpec as P

tap_group = 16


def from_behind(array, axis, by):
    count = lax.axis_size(axis)
    pairs = [(i, i + by) for i in range(count) if 0 <= i + by < count]
    return lax.ppermute(array, axis, pairs)


def doc_starts(bound_row, positions):
    below = bound_row[None, :] <= positions[:, None]
    return jnp.max(jnp.where(below, bound_row[None, :], 0), axis=1)


def shards(query_gate, key_proj, value_proj, grad_out, filters, doc_bounds, continues):
    weights = lax.all_gather(filters, "fsdp", axis=0, tiled=True)
    filter_len = weights.shape[0]
    length = query_gate.shape[1]
    shard_index = lax.axis_index("ctx")
    first_token = shard_index * length
    positions = first_token + jnp.arange(length, dtype=jnp.int32)
    bound_row = doc_bounds[0]
    own_flag = continues[0, 0]
    plain_starts = doc_starts(bound_row, positions)
    own_starts = jnp.where(own_flag == 1, plain_starts, jnp.maximum(plain_starts, first_token))
    later_positions = first_token + length + jnp.arange(filter_len, dtype=jnp.int32)
    reach_starts = jnp.concatenate([own_starts, doc_starts(bound_row, later_positions)])
    query_local = query_gate[0]
    key_local = key_proj[0]
    value_local = value_proj[0]
    grad_local = grad_out[0]
    channels = query_local.shape[1]
    mixed_input = (key_local.astype(jnp.float32) * value_local.astype(jnp.float32)).astype(
        jnp.bfloat16
    )
    rows_before = from_behind(mixed_input, "ctx", 1)
    mixed_ext = jnp.concatenate([rows_before, mixed_input], axis=0)
    grad_conv = (grad_local.astype(jnp.float32) * query_local.astype(jnp.float32)).astype(
        jnp.bfloat16
    )
    send_rows = jnp.where(own_flag == 1, grad_conv, jnp.zeros_like(grad_conv))
    rows_after = from_behind(send_rows, "ctx", -1)
    grad_ext = jnp.concatenate([grad_conv, rows_after], axis=0)
    grad_wide = grad_conv.astype(jnp.float32)

    def tap_block(group_index, state_tuple):
        conv_out, grad_back, filt_grad = state_tuple
        for offset in range(tap_group):
            tap_index = group_index * tap_group + offset
            weight_row = lax.dynamic_slice_in_dim(weights, tap_index, 1, 0)
            earlier = lax.dynamic_slice_in_dim(mixed_ext, filter_len - tap_index, length, 0).astype(
                jnp.float32
            )
            inside = (positions - tap_index >= own_starts)[:, None]
            conv_out = conv_out + jnp.where(inside, earlier * weight_row, 0.0)
            tap_term = jnp.sum(jnp.where(inside, grad_wide * earlier, 0.0), axis=0)
            filt_grad = lax.dynamic_update_slice_in_dim(filt_grad, tap_term[None, :], tap_index, 0)
            ahead_rows = lax.dynamic_slice_in_dim(grad_ext, tap_index, length, 0).astype(
                jnp.float32
            )
            reaching = (positions >= lax.dynamic_slice_in_dim(reach_starts, tap_index, length, 0))[
                :, None
            ]
            grad_back = grad_back + jnp.where(reaching, ahead_rows * weight_row, 0.0)
        return (conv_out, grad_back, filt_grad)

    start_state = (
        jnp.zeros((length, channels), jnp.float32),
        jnp.zeros((length, channels), jnp.float32),
        jnp.zeros((filter_len, channels), jnp.float32),
    )
    conv_out, grad_back, filt_grad = lax.fori_loop(
        jnp.int32(0), jnp.int32(filter_len // tap_group), tap_block, start_state
    )
    grad_query = (grad_local.astype(jnp.float32) * conv_out).astype(jnp.bfloat16)
    grad_key = (grad_back * value_local.astype(jnp.float32)).astype(jnp.bfloat16)
    grad_value = (grad_back * key_local.astype(jnp.float32)).astype(jnp.bfloat16)
    norm_scale = 1.0 / math.sqrt(lax.axis_size("fsdp") * lax.axis_size("ctx") * length)
    filt_grad = filt_grad * norm_scale
    summed_all = lax.psum(filt_grad, "ctx")
    share_out = lax.psum_scatter(summed_all, "fsdp", scatter_dimension=0, tiled=True)
    return (grad_query[None], grad_key[None], grad_value[None], share_out)


def solution(mesh):
    in_specs = (
        P("fsdp", "ctx", "tp"),
        P("fsdp", "ctx", "tp"),
        P("fsdp", "ctx", "tp"),
        P("fsdp", "ctx", "tp"),
        P("fsdp", "tp"),
        P("fsdp", None),
        P("fsdp", "ctx"),
    )
    out_specs = (
        P("fsdp", "ctx", "tp"),
        P("fsdp", "ctx", "tp"),
        P("fsdp", "ctx", "tp"),
        P("fsdp", "tp"),
    )
    return jax.shard_map(shards, mesh=mesh, in_specs=in_specs, out_specs=out_specs, check_vma=False)
```

profile of v0, /device:TPU:1, one launch (start us, length us, event | category | flops | bytes accessed | tf_op | source)
XLA Modules:
  0.0 783.8 jit_solution(15440662783563626389)
XLA Ops:
  8.0 1.9 fusion.132
  9.9 4.5 collective-permute-start
  17.7 2.9 collective-permute-start.1
  20.8 5.3 collective-permute-done
  26.1 1.8 pad_maximum_fusion
  28.0 6.5 collective-permute-done.1
  34.4 2.8 pad_maximum_fusion.1
  37.2 25.2 %all-gather.2.cloned.1.call-done = f32[128,4096]{1,0:T(8,128)} async-done(((f32[32,4096]{1,0:T(8,128)}), f32[128,4096]{1,0:T(8,128)}) %all-gather.2.cloned.1.call-update) | async-done | bytes 2097168 | tf_op jit(solution)/shard_map/all_gather | solution.py:23
  63.9 540.4 %while.18 = (s32[]{:T(128)}, f32[128,4096]{1,0:T(8,128)}, f32[128,4096]{1,0:T(8,128)}, f32[128,4096]{1,0:T(8,128)}, s32[128]{0:T(128)S(1)}, /*index=5*/bf16[256,...) while((s32[]{:T(128)}, f32[128,4096]{1,0:T(8,128)}, ...), condition=%wide.region_19.20_spmd.clone, body=%wide.region_2.19_spmd.clone.sunk | while | flops 101652864 | bytes 89937200 | solution.py:79
  64.1 6.7 fusion.150
  70.8 5.3 fusion.149
  76.1 2.4 constant_dynamic-slice_fusion.17
  104.1 15.4 %fusion.148 = f32[128,4096]{1,0:T(8,128)} fusion(f32[128,4096]{1,0:T(8,128)} %get-tuple-element.669, bf16[256,4096]{1,0:T(8,128)(2,1)} %get-tuple-element.736, s32[]{:T(128)S(6)} %select_n.1126, s32[]{:T(128)S(6)} %select_n.1127, s32[]{:T(128)S(6)} %select_n.1128, s32[]{:T(128)S(6)} %select_n.1129, s32[]{:T(128)S(6)} %select_n.1130, ...), kind=kLoop, calls=%fused_computation.112.clone.1 | loop fusion | flops 34078720 | bytes 21235776 | tf_op jit(solution)/shard_map/while/body/add | solution.py:71
  119.5 10.1 %fusion.146 = f32[128,4096]{1,0:T(8,128)S(1)} fusion(f32[128,4096]{1,0:T(8,128)S(1)} %copy-done.2, f32[4096]{0:T(1024)S(1)} %bitcast.124, f32[4096]{0:T(1024)S(1)} %bitcast.126, f32[4096]{0:T(1024)S(1)} %bitcast.128, f32[4096]{0:T(1024)S(1)} %bitcast.130, f32[4096]{0:T(1024)S(1)} %bitcast.132, f32[4096]{0:T(1024)S(1)} %bitcast.134, ...), kind=kLoop, calls=%fused_computation.49.clone.1 | loop fusion | flops 34078720 | bytes 21235776 | tf_op jit(solution)/shard_map/while/body/add | solution.py:62
  131.2 6.7 fusion.150
  137.9 5.3 fusion.149
  143.2 2.4 constant_dynamic-slice_fusion.17
  171.3 15.7 %fusion.148 = f32[128,4096]{1,0:T(8,128)} fusion(f32[128,4096]{1,0:T(8,128)} %get-tuple-element.669, bf16[256,4096]{1,0:T(8,128)(2,1)} %get-tuple-element.736, s32[]{:T(128)S(6)} %select_n.1126, s32[]{:T(128)S(6)} %select_n.1127, s32[]{:T(128)S(6)} %select_n.1128, s32[]{:T(128)S(6)} %select_n.1129, s32[]{:T(128)S(6)} %select_n.1130, ...), kind=kLoop, calls=%fused_computation.112.clone.1 | loop fusion | flops 34078720 | bytes 21235776 | tf_op jit(solution)/shard_map/while/body/add | solution.py:71
  187.1 10.1 %fusion.146 = f32[128,4096]{1,0:T(8,128)S(1)} fusion(f32[128,4096]{1,0:T(8,128)S(1)} %copy-done.2, f32[4096]{0:T(1024)S(1)} %bitcast.124, f32[4096]{0:T(1024)S(1)} %bitcast.126, f32[4096]{0:T(1024)S(1)} %bitcast.128, f32[4096]{0:T(1024)S(1)} %bitcast.130, f32[4096]{0:T(1024)S(1)} %bitcast.132, f32[4096]{0:T(1024)S(1)} %bitcast.134, ...), kind=kLoop, calls=%fused_computation.49.clone.1 | loop fusion | flops 34078720 | bytes 21235776 | tf_op jit(solution)/shard_map/while/body/add | solution.py:62
  198.7 6.7 fusion.150
  205.4 5.3 fusion.149
  210.7 2.4 constant_dynamic-slice_fusion.17
  213.2 1.6 dynamic_update_slice.144
  238.9 15.9 %fusion.148 = f32[128,4096]{1,0:T(8,128)} fusion(f32[128,4096]{1,0:T(8,128)} %get-tuple-element.669, bf16[256,4096]{1,0:T(8,128)(2,1)} %get-tuple-element.736, s32[]{:T(128)S(6)} %select_n.1126, s32[]{:T(128)S(6)} %select_n.1127, s32[]{:T(128)S(6)} %select_n.1128, s32[]{:T(128)S(6)} %select_n.1129, s32[]{:T(128)S(6)} %select_n.1130, ...), kind=kLoop, calls=%fused_computation.112.clone.1 | loop fusion | flops 34078720 | bytes 21235776 | tf_op jit(solution)/shard_map/while/body/add | solution.py:71
  254.9 10.1 %fusion.146 = f32[128,4096]{1,0:T(8,128)S(1)} fusion(f32[128,4096]{1,0:T(8,128)S(1)} %copy-done.2, f32[4096]{0:T(1024)S(1)} %bitcast.124, f32[4096]{0:T(1024)S(1)} %bitcast.126, f32[4096]{0:T(1024)S(1)} %bitcast.128, f32[4096]{0:T(1024)S(1)} %bitcast.130, f32[4096]{0:T(1024)S(1)} %bitcast.132, f32[4096]{0:T(1024)S(1)} %bitcast.134, ...), kind=kLoop, calls=%fused_computation.49.clone.1 | loop fusion | flops 34078720 | bytes 21235776 | tf_op jit(solution)/shard_map/while/body/add | solution.py:62
  266.5 6.7 fusion.150
  273.2 5.3 fusion.149
  278.5 2.4 constant_dynamic-slice_fusion.17
  306.4 16.0 %fusion.148 = f32[128,4096]{1,0:T(8,128)} fusion(f32[128,4096]{1,0:T(8,128)} %get-tuple-element.669, bf16[256,4096]{1,0:T(8,128)(2,1)} %get-tuple-element.736, s32[]{:T(128)S(6)} %select_n.1126, s32[]{:T(128)S(6)} %select_n.1127, s32[]{:T(128)S(6)} %select_n.1128, s32[]{:T(128)S(6)} %select_n.1129, s32[]{:T(128)S(6)} %select_n.1130, ...), kind=kLoop, calls=%fused_computation.112.clone.1 | loop fusion | flops 34078720 | bytes 21235776 | tf_op jit(solution)/shard_map/while/body/add | solution.py:71
  322.5 10.1 %fusion.146 = f32[128,4096]{1,0:T(8,128)S(1)} fusion(f32[128,4096]{1,0:T(8,128)S(1)} %copy-done.2, f32[4096]{0:T(1024)S(1)} %bitcast.124, f32[4096]{0:T(1024)S(1)} %bitcast.126, f32[4096]{0:T(1024)S(1)} %bitcast.128, f32[4096]{0:T(1024)S(1)} %bitcast.130, f32[4096]{0:T(1024)S(1)} %bitcast.132, f32[4096]{0:T(1024)S(1)} %bitcast.134, ...), kind=kLoop, calls=%fused_computation.49.clone.1 | loop fusion | flops 34078720 | bytes 21235776 | tf_op jit(solution)/shard_map/while/body/add | solution.py:62
  334.1 6.7 fusion.150
  340.8 5.3 fusion.149
  346.1 2.4 constant_dynamic-slice_fusion.17
  374.2 15.8 %fusion.148 = f32[128,4096]{1,0:T(8,128)} fusion(f32[128,4096]{1,0:T(8,128)} %get-tuple-element.669, bf16[256,4096]{1,0:T(8,128)(2,1)} %get-tuple-element.736, s32[]{:T(128)S(6)} %select_n.1126, s32[]{:T(128)S(6)} %select_n.1127, s32[]{:T(128)S(6)} %select_n.1128, s32[]{:T(128)S(6)} %select_n.1129, s32[]{:T(128)S(6)} %select_n.1130, ...), kind=kLoop, calls=%fused_computation.112.clone.1 | loop fusion | flops 34078720 | bytes 21235776 | tf_op jit(solution)/shard_map/while/body/add | solution.py:71
  390.0 10.1 %fusion.146 = f32[128,4096]{1,0:T(8,128)S(1)} fusion(f32[128,4096]{1,0:T(8,128)S(1)} %copy-done.2, f32[4096]{0:T(1024)S(1)} %bitcast.124, f32[4096]{0:T(1024)S(1)} %bitcast.126, f32[4096]{0:T(1024)S(1)} %bitcast.128, f32[4096]{0:T(1024)S(1)} %bitcast.130, f32[4096]{0:T(1024)S(1)} %bitcast.132, f32[4096]{0:T(1024)S(1)} %bitcast.134, ...), kind=kLoop, calls=%fused_computation.49.clone.1 | loop fusion | flops 34078720 | bytes 21235776 | tf_op jit(solution)/shard_map/while/body/add | solution.py:62
  401.6 6.7 fusion.150
  408.3 5.3 fusion.149
  413.6 2.4 constant_dynamic-slice_fusion.17
  441.6 15.6 %fusion.148 = f32[128,4096]{1,0:T(8,128)} fusion(f32[128,4096]{1,0:T(8,128)} %get-tuple-element.669, bf16[256,4096]{1,0:T(8,128)(2,1)} %get-tuple-element.736, s32[]{:T(128)S(6)} %select_n.1126, s32[]{:T(128)S(6)} %select_n.1127, s32[]{:T(128)S(6)} %select_n.1128, s32[]{:T(128)S(6)} %select_n.1129, s32[]{:T(128)S(6)} %select_n.1130, ...), kind=kLoop, calls=%fused_computation.112.clone.1 | loop fusion | flops 34078720 | bytes 21235776 | tf_op jit(solution)/shard_map/while/body/add | solution.py:71
  457.3 10.1 %fusion.146 = f32[128,4096]{1,0:T(8,128)S(1)} fusion(f32[128,4096]{1,0:T(8,128)S(1)} %copy-done.2, f32[4096]{0:T(1024)S(1)} %bitcast.124, f32[4096]{0:T(1024)S(1)} %bitcast.126, f32[4096]{0:T(1024)S(1)} %bitcast.128, f32[4096]{0:T(1024)S(1)} %bitcast.130, f32[4096]{0:T(1024)S(1)} %bitcast.132, f32[4096]{0:T(1024)S(1)} %bitcast.134, ...), kind=kLoop, calls=%fused_computation.49.clone.1 | loop fusion | flops 34078720 | bytes 21235776 | tf_op jit(solution)/shard_map/while/body/add | solution.py:62
  468.9 6.7 fusion.150
  475.6 5.3 fusion.149
  480.9 2.4 constant_dynamic-slice_fusion.17
  508.9 16.1 %fusion.148 = f32[128,4096]{1,0:T(8,128)} fusion(f32[128,4096]{1,0:T(8,128)} %get-tuple-element.669, bf16[256,4096]{1,0:T(8,128)(2,1)} %get-tuple-element.736, s32[]{:T(128)S(6)} %select_n.1126, s32[]{:T(128)S(6)} %select_n.1127, s32[]{:T(128)S(6)} %select_n.1128, s32[]{:T(128)S(6)} %select_n.1129, s32[]{:T(128)S(6)} %select_n.1130, ...), kind=kLoop, calls=%fused_computation.112.clone.1 | loop fusion | flops 34078720 | bytes 21235776 | tf_op jit(solution)/shard_map/while/body/add | solution.py:71
  525.0 10.1 %fusion.146 = f32[128,4096]{1,0:T(8,128)S(1)} fusion(f32[128,4096]{1,0:T(8,128)S(1)} %copy-done.2, f32[4096]{0:T(1024)S(1)} %bitcast.124, f32[4096]{0:T(1024)S(1)} %bitcast.126, f32[4096]{0:T(1024)S(1)} %bitcast.128, f32[4096]{0:T(1024)S(1)} %bitcast.130, f32[4096]{0:T(1024)S(1)} %bitcast.132, f32[4096]{0:T(1024)S(1)} %bitcast.134, ...), kind=kLoop, calls=%fused_computation.49.clone.1 | loop fusion | flops 34078720 | bytes 21235776 | tf_op jit(solution)/shard_map/while/body/add | solution.py:62
  536.6 6.7 fusion.150
  543.3 5.3 fusion.149
  548.6 2.4 constant_dynamic-slice_fusion.17
  563.9 1.6 dynamic_update_slice.152
  565.5 1.6 dynamic_update_slice.153
  567.1 1.6 dynamic_update_slice.154
  568.7 1.6 dynamic_update_slice.155
  570.4 1.6 dynamic_update_slice.156
  572.0 1.6 dynamic_update_slice.157
  573.6 1.6 dynamic_update_slice.158
  575.2 1.6 dynamic_update_slice.159
  576.9 16.1 %fusion.148 = f32[128,4096]{1,0:T(8,128)} fusion(f32[128,4096]{1,0:T(8,128)} %get-tuple-element.669, bf16[256,4096]{1,0:T(8,128)(2,1)} %get-tuple-element.736, s32[]{:T(128)S(6)} %select_n.1126, s32[]{:T(128)S(6)} %select_n.1127, s32[]{:T(128)S(6)} %select_n.1128, s32[]{:T(128)S(6)} %select_n.1129, s32[]{:T(128)S(6)} %select_n.1130, ...), kind=kLoop, calls=%fused_computation.112.clone.1 | loop fusion | flops 34078720 | bytes 21235776 | tf_op jit(solution)/shard_map/while/body/add | solution.py:71
  592.9 10.1 %fusion.146 = f32[128,4096]{1,0:T(8,128)S(1)} fusion(f32[128,4096]{1,0:T(8,128)S(1)} %copy-done.2, f32[4096]{0:T(1024)S(1)} %bitcast.124, f32[4096]{0:T(1024)S(1)} %bitcast.126, f32[4096]{0:T(1024)S(1)} %bitcast.128, f32[4096]{0:T(1024)S(1)} %bitcast.130, f32[4096]{0:T(1024)S(1)} %bitcast.132, f32[4096]{0:T(1024)S(1)} %bitcast.134, ...), kind=kLoop, calls=%fused_computation.49.clone.1 | loop fusion | flops 34078720 | bytes 21235776 | tf_op jit(solution)/shard_map/while/body/add | solution.py:62
  604.4 3.2 broadcast_multiply_fusion
  609.2 3.1 fusion.134
  612.3 47.3 %reduce-scatter.2.cloned.1.call-done = f32[32,4096]{1,0:T(8,128)} async-done(((f32[128,4096]{1,0:T(8,128)}), f32[32,4096]{1,0:T(8,128)}) %reduce-scatter.2.cloned.1.call-update) | async-done | bytes 524304 | tf_op jit(solution)/shard_map/reduce_scatter | solution.py:88
  659.6 3.0 fusion.136
  662.6 112.8 %all-reduce.2.cloned.1.call-done = f32[32,4096]{1,0:T(8,128)} async-done(((f32[32,4096]{1,0:T(8,128)}), f32[32,4096]{1,0:T(8,128)}) %all-reduce.2.cloned.1.call-update) | async-done | bytes 524304 | tf_op jit(solution)/shard_map/psum | solution.py:87
  775.4 1.9 copy.41
  (210 shorter events, 209.2 us)
Async XLA Ops:
  7.2 7.9 %copy-start.5 = (bf16[1,128,4096]{2,1,0:T(8,128)(2,1)S(1)}, bf16[1,128,4096]{2,1,0:T(8,128)(2,1)}, u32[]{:S(2)}) copy-start(bf16[1,128,4096]{2,1,0:T(8,128)(2,1)} %param.12) | copy-start | bytes 3145732
  7.2 55.2 %all-gather.2.cloned.1.call-start = ((), (), s32[]{:S(2)}) async-start(), calls=%async_computation.1 | async-start | bytes 2621440 | tf_op jit(solution)/shard_map/all_gather | solution.py:23
  7.9 651.6 %reduce-scatter.2.cloned.1.call-start = ((), (), s32[]{:S(2)}) async-start(), calls=%async_computation.2 | async-start | bytes 2621440 | tf_op jit(solution)/shard_map/reduce_scatter | solution.py:88
  8.0 7.1 copy-start.7
  9.8 6.8 copy-start.6
  9.9 16.2 %collective-permute-start = (bf16[128,4096]{1,0:T(8,128)(2,1)S(1)}, bf16[128,4096]{1,0:T(8,128)(2,1)}, u32[]{:S(2)}, u32[]{:S(2)}) collective-permute-start(bf16[128,4096]{1,0:T(8,128)(2,1)S(1)} %fusion.132), channel_id=1, source_target_pairs={{0,8},{8,16},{16,24},{24,32},{32,40},{40,48},{48,56},{56,64},{64,7... | collective-permute-start | bytes 3145736 | tf_op jit(solution)/shard_map/ppermute | solution.py:14
  16.7 4.0 copy-start.8
  17.7 16.7 %collective-permute-start.1 = (bf16[128,4096]{1,0:T(8,128)(2,1)}, bf16[128,4096]{1,0:T(8,128)(2,1)}, u32[]{:S(2)}, u32[]{:S(2)}) collective-permute-start(bf16[128,4096]{1,0:T(8,128)(2,1)} %broadcast_select_fusion), channel_id=1, source_target_pairs={{8,0},{16,8},{24,16},{32,24},{40,32},{48,40},{56,48},{64,56},{72,6... | collective-permute-start | bytes 3145736 | tf_op jit(solution)/shard_map/ppermute | solution.py:14
  64.1 6.7 copy-start
  104.1 15.4 %copy-start.2 = (f32[128,4096]{1,0:T(8,128)S(1)}, f32[128,4096]{1,0:T(8,128)}, u32[]{:S(2)}) copy-start(f32[128,4096]{1,0:T(8,128)} %get-tuple-element.668) | copy-start | bytes 6291460 | tf_op jit(solution)/shard_map/while
  129.7 1.3 copy-start.3
  131.2 6.7 copy-start
  171.3 15.7 %copy-start.2 = (f32[128,4096]{1,0:T(8,128)S(1)}, f32[128,4096]{1,0:T(8,128)}, u32[]{:S(2)}) copy-start(f32[128,4096]{1,0:T(8,128)} %get-tuple-element.668) | copy-start | bytes 6291460 | tf_op jit(solution)/shard_map/while
  197.2 1.3 copy-start.3
  198.7 6.7 copy-start
  238.9 15.9 %copy-start.2 = (f32[128,4096]{1,0:T(8,128)S(1)}, f32[128,4096]{1,0:T(8,128)}, u32[]{:S(2)}) copy-start(f32[128,4096]{1,0:T(8,128)} %get-tuple-element.668) | copy-start | bytes 6291460 | tf_op jit(solution)/shard_map/while
  265.0 1.3 copy-start.3
  266.5 6.7 copy-start
  306.4 16.1 %copy-start.2 = (f32[128,4096]{1,0:T(8,128)S(1)}, f32[128,4096]{1,0:T(8,128)}, u32[]{:S(2)}) copy-start(f32[128,4096]{1,0:T(8,128)} %get-tuple-element.668) | copy-start | bytes 6291460 | tf_op jit(solution)/shard_map/while
  332.6 1.3 copy-start.3
  334.1 6.7 copy-start
  374.2 15.8 %copy-start.2 = (f32[128,4096]{1,0:T(8,128)S(1)}, f32[128,4096]{1,0:T(8,128)}, u32[]{:S(2)}) copy-start(f32[128,4096]{1,0:T(8,128)} %get-tuple-element.668) | copy-start | bytes 6291460 | tf_op jit(solution)/shard_map/while
  400.1 1.3 copy-start.3
  401.6 6.7 copy-start
  441.6 15.6 %copy-start.2 = (f32[128,4096]{1,0:T(8,128)S(1)}, f32[128,4096]{1,0:T(8,128)}, u32[]{:S(2)}) copy-start(f32[128,4096]{1,0:T(8,128)} %get-tuple-element.668) | copy-start | bytes 6291460 | tf_op jit(solution)/shard_map/while
  467.4 1.3 copy-start.3
  468.9 6.7 copy-start
  508.9 16.1 %copy-start.2 = (f32[128,4096]{1,0:T(8,128)S(1)}, f32[128,4096]{1,0:T(8,128)}, u32[]{:S(2)}) copy-start(f32[128,4096]{1,0:T(8,128)} %get-tuple-element.668) | copy-start | bytes 6291460 | tf_op jit(solution)/shard_map/while
  535.1 1.3 copy-start.3
  536.6 6.7 copy-start
  576.9 16.1 %copy-start.2 = (f32[128,4096]{1,0:T(8,128)S(1)}, f32[128,4096]{1,0:T(8,128)}, u32[]{:S(2)}) copy-start(f32[128,4096]{1,0:T(8,128)} %get-tuple-element.668) | copy-start | bytes 6291460 | tf_op jit(solution)/shard_map/while
  603.0 1.3 copy-start.3
  604.4 3.3 copy-start.4
  607.6 1.6 copy-start.1
  607.6 167.7 %all-reduce.2.cloned.1.call-start = ((), (), s32[]{:S(2)}) async-start(), calls=%async_computation.3 | async-start | bytes 1048576 | tf_op jit(solution)/shard_map/psum | solution.py:87
Sparse Core Ops, SparseCore 0:
  9.8 52.5 all-gather.1
  607.7 51.7 reduce-scatter.1
  663.0 112.2 all-reduce.1
where the time goes:
time: 787 us; the launch traced here: 784 us
  other arithmetic  323 us (41%)
  local copies, waits for them, and re-layouts  240 us (30%)
  waiting for transfers between devices  198 us (25%)
  between operations  14.5 us (2%)
    dynamic_update_slice x128, local copies, waits for them, and re-layouts, tap_block(): lax.dynamic_update_slice_in_dim(filt_grad, tap_term[None, :], tap_index, 0)  205 us
    add x8, other arithmetic, tap_block(): grad_back = grad_back + jnp.where(reaching, ahead_rows * weight_row, 0.0)  127 us
    psum x1, waiting for transfers between devices, shards(): summed_all = lax.psum(filt_grad, 'ctx')  113 us
    reduce_sum x16, other arithmetic, tap_block(): tap_term = jnp.sum(jnp.where(inside, grad_wide * earlier, 0.0), axis=0)  95.8 us
    add x8, other arithmetic, tap_block(): conv_out = conv_out + jnp.where(inside, earlier * weight_row, 0.0)  80.8 us
    reduce_scatter x1, waiting for transfers between devices, shards(): lax.psum_scatter(summed_all, 'fsdp', scatter_dimension=0, tiled=True)  47.3 us
    all_gather x1, waiting for transfers between devices, shards(): weights = lax.all_gather(filters, 'fsdp', axis=0, tiled=True)  25.2 us
    dynamic_slice x8, local copies, waits for them, and re-layouts, tap_block(): weight_row = lax.dynamic_slice_in_dim(weights, tap_index, 1, 0)  19.3 us
  transfers between devices with their start and end apart: 5, of which 5 were waited for; matrix products, arithmetic and copies ran while one was open for 2% of the time, Pallas kernels for 0%

commit v1 on v0

v1 whole, which is shorter than its diff:
```python
import functools
import math

import jax
import jax.numpy as jnp
import numpy as np
from jax import lax
from jax.experimental import pallas as pl
from jax.experimental.pallas import tpu as pltpu
from jax.sharding import PartitionSpec as P

MESH = pl.DeviceIdType.MESH
T = 128
CW = 512
F32 = jnp.float32
BF16 = jnp.bfloat16
NY, NX, NCORE, NF = 4, 4, 2, 4
BIG = 1e6


def tables():
    theta = np.pi * (np.arange(T) + 0.5)[:, None] / T
    point = np.arange(T)[None, :]

    def pair(offset):
        return np.concatenate([np.cos(theta * (point + offset)), -np.sin(theta * (point + offset))], axis=0)

    forward = pair(0)
    conv_back = pair(T).T / T
    grad_back = pair(-T).T / T
    return [forward.astype(np.float32), conv_back.astype(np.float32), grad_back.astype(np.float32)]


def turn_cos(u):
    u = u - jnp.floor(u + 0.5)
    z = u * u
    total = None
    for n in range(8, -1, -1):
        c = (-1.0) ** n * (2 * math.pi) ** (2 * n) / math.factorial(2 * n)
        total = jnp.full_like(z, c) if total is None else total * z + c
    return total


def turn_sin(u):
    u = u - jnp.floor(u + 0.5)
    z = u * u
    total = None
    for n in range(8, -1, -1):
        c = (-1.0) ** n * (2 * math.pi) ** (2 * n + 1) / math.factorial(2 * n + 1)
        total = jnp.full_like(z, c) if total is None else total * z + c
    return total * u


def dot(a, b):
    return jnp.dot(a, b, preferred_element_type=F32)


def kernel(n_ctx, norm, bounds_ref, cont_ref, fwd_ref, cback_ref, gback_ref, filt_ref, k_hbm, v_hbm, q_hbm, o_hbm,
           gq_hbm, gk_hbm, gv_hbm, gf_ref,
           kb, vb, qb, ob, xb, gb, gm, xp, gn, wb, oq, ok, ov, gfb, r0, p0, r1, p1, r2, p2, r3, fin, r4,
           xg_m, w_m, xp_m, gn_m, conv_m, grad_m, filt_m,
           in_sem, out_sem, hs_sem, hr_sem, ws1, wr1, ws2, wr2, ws3, wr3,
           s0, q0, s1, q1, s2, q2, s3, q3, s4, q4):
    n_chunk = xb.shape[0]
    n_super = n_chunk // 2
    ctx = lax.axis_index("ctx")
    fs = lax.axis_index("fsdp")
    core = lax.rem(ctx, NCORE)
    xi = lax.rem(ctx // NCORE, NX)
    yi = ctx // (NCORE * NX)

    def at(y, x, c):
        return {"ctx": (y * NX + x) * NCORE + c}

    def y_of(d):
        return lax.rem(yi + d, NY)

    def x_of(d):
        return lax.rem(xi + d, NX)

    def f_of(d):
        return lax.rem(fs + d, NF)

    nxt = {"ctx": lax.rem(ctx + 1, n_ctx)}
    prv = {"ctx": lax.rem(ctx + n_ctx - 1, n_ctx)}
    mate = at(yi, xi, 1 - core)
    peers = [nxt, prv, mate]
    peers += [{"fsdp": f_of(d)} for d in (1, 2, 3)]
    peers += [at(y_of(d), xi, c) for d in (1, 2, 3) for c in (core, 1 - core)]
    peers += [at(yi, x_of(d), core) for d in (1, 2, 3)]

    def loads(j):
        cols = pl.ds(pl.multiple_of(j * CW, CW), CW)
        return [pltpu.make_async_copy(src.at[:, cols], dst.at[j], in_sem.at[i, j])
                for i, (src, dst) in enumerate(((k_hbm, kb), (v_hbm, vb), (q_hbm, qb), (o_hbm, ob)))]

    @pl.loop(0, n_chunk)
    def _(j):
        for copy in loads(j):
            copy.start()

    barrier = pltpu.get_barrier_semaphore()
    for peer in peers:
        pl.semaphore_signal(barrier, inc=1, device_id=peer, device_id_type=MESH)

    first = (ctx * T).astype(F32)
    bounds = bounds_ref[...].astype(F32)
    flag = cont_ref[...] == 1
    row = lax.broadcasted_iota(jnp.int32, (T, 1), 0).astype(F32)
    lane = lax.broadcasted_iota(jnp.int32, (1, T), 1).astype(F32)
    low = jnp.max(jnp.where(bounds <= row + first, bounds, 0.0), axis=1, keepdims=True)
    high = jnp.min(jnp.where(bounds > row + first, bounds, BIG), axis=1, keepdims=True)
    begin = jnp.maximum(low - first, 0.0)
    end = jnp.minimum(high - first, float(T))
    size = end - begin
    first_cut = jnp.min(jnp.where(bounds >= first, bounds, BIG), axis=1, keepdims=True) - first
    prev_start = jnp.max(jnp.where(bounds <= first, bounds, 0.0), axis=1, keepdims=True) - first + T
    last_start = jnp.max(jnp.where(bounds <= first + (T - 1), bounds, 0.0), axis=1, keepdims=True) - first
    head_row = jnp.logical_and(row < first_cut, flag)
    tail_row = row >= last_start
    prev_lane = lane >= prev_start
    head_lane = jnp.logical_and(lane < first_cut, flag)

    freq = (row - begin + 0.5) / (2.0 * size)
    same = jnp.logical_and(lane >= begin, lane < end)
    turn = freq * (lane - begin)
    a_re = jnp.where(same, turn_cos(turn), 0.0)
    a_im = jnp.where(same, -turn_sin(turn), 0.0)
    short = lane < size
    turn = freq * lane
    b_re = jnp.where(short, turn_cos(turn), 0.0) / size
    b_im = jnp.where(short, -turn_sin(turn), 0.0) / size
    fwd = fwd_ref[...]
    fwd16 = fwd.astype(BF16)
    xg_m[0:T, :] = a_re.astype(BF16)
    xg_m[T:2 * T, :] = a_im.astype(BF16)
    xg_m[2 * T:4 * T, :] = jnp.where(head_lane, fwd, 0.0).astype(BF16)
    w_m[0:T, :] = b_re.astype(BF16)
    w_m[T:2 * T, :] = b_im.astype(BF16)
    w_m[2 * T:4 * T, :] = fwd16
    xp_m[...] = jnp.where(prev_lane, fwd, 0.0).astype(BF16)
    gn_m[...] = fwd16
    a_back = [a_re.T.astype(BF16), a_im.T.astype(BF16)]
    for m in (conv_m, grad_m):
        m[:, 0:T] = a_back[0]
        m[:, T:2 * T] = a_back[1]
    conv_m[:, 2 * T:4 * T] = jnp.where(head_row, cback_ref[...], 0.0).astype(BF16)
    grad_m[:, 2 * T:4 * T] = jnp.where(tail_row, gback_ref[...], 0.0).astype(BF16)
    filt_m[:, 0:T] = (b_re * norm).T.astype(BF16)
    filt_m[:, T:2 * T] = (b_im * norm).T.astype(BF16)
    filt_m[:, 2 * T:4 * T] = (gback_ref[...] * norm).astype(BF16)

    pl.semaphore_wait(barrier, len(peers))

    own = yi * NCORE + core
    taps = T // NF
    own_rows = pl.ds(pl.multiple_of(fs * taps, taps), taps)
    own_cols = pl.ds(pl.multiple_of(own * CW, CW), CW)
    wb[own, own_rows, :] = filt_ref[:, own_cols].astype(BF16)

    def w_copy(chunk_ref_src, chunk_ref_dst, s, r, dev):
        return pltpu.make_async_remote_copy(src_ref=chunk_ref_src, dst_ref=chunk_ref_dst, send_sem=s, recv_sem=r,
                                            device_id=dev, device_id_type=MESH)

    pending = []
    stage1 = []
    for d in (1, 2, 3):
        copy = w_copy(wb.at[own, own_rows, :], wb.at[own, own_rows, :], ws1.at[d - 1], wr1.at[d - 1], {"fsdp": f_of(d)})
        copy.start()
        stage1.append(copy)

    def halo(j):
        return [w_copy(xb.at[j], xp.at[j], hs_sem.at[0, j], hr_sem.at[0, j], nxt),
                w_copy(gm.at[j], gn.at[j], hs_sem.at[1, j], hr_sem.at[1, j], prv)]

    @pl.loop(0, n_chunk)
    def _(j):
        for copy in loads(j):
            copy.wait()
        xb[j] = (kb[j].astype(F32) * vb[j].astype(F32)).astype(BF16)
        grad_conv = (ob[j].astype(F32) * qb[j].astype(F32)).astype(BF16)
        gb[j] = grad_conv
        gm[j] = jnp.where(head_row, grad_conv.astype(F32), 0.0).astype(BF16)
        for copy in halo(j):
            copy.start()

    for copy in stage1:
        copy.wait()
    stage2 = []
    for d in (1, 2, 3):
        copy = w_copy(wb.at[own], wb.at[own], ws2.at[d - 1], wr2.at[d - 1], at(y_of(d), xi, core))
        copy.start()
        stage2.append(copy)
    stage3 = [w_copy(wb.at[own], wb.at[own], ws3.at[0], wr3.at[0], mate)]
    stage3[0].start()
    for d in (1, 2, 3):
        stage2[d - 1].wait_recv()
        got = lax.rem(yi + NY - d, NY) * NCORE + core
        copy = w_copy(wb.at[got], wb.at[got], ws3.at[d], wr3.at[d], mate)
        copy.start()
        stage3.append(copy)
    for copy in stage3:
        copy.wait_recv()

    def stores(j):
        cols = pl.ds(pl.multiple_of(j * CW, CW), CW)
        return [pltpu.make_async_copy(src.at[j], dst.at[:, cols], out_sem.at[i, j])
                for i, (src, dst) in enumerate(((oq, gq_hbm), (ok, gk_hbm), (ov, gv_hbm)))]

    def times(a, b):
        return [(a[0] * b[0] - a[1] * b[1]).astype(BF16), (a[0] * b[1] + a[1] * b[0]).astype(BF16)]

    def times_conj(a, b):
        return [(a[0] * b[0] + a[1] * b[1]).astype(BF16), (a[1] * b[0] - a[0] * b[1]).astype(BF16)]

    def halves(a):
        return [a[0:T], a[T:2 * T]]

    def chunk(j):
        for copy in halo(j):
            copy.wait_recv()
        for c in range(0, CW, 256):
            cols = pl.ds(c, 256)
            x_in = halves(dot(xg_m[0:2 * T, :], xb[j, :, cols]))
            g_all = dot(xg_m[...], gb[j, :, cols])
            w_all = dot(w_m[...], wb[j, :, cols])
            g_in, g_edge = halves(g_all[0:2 * T]), halves(g_all[2 * T:])
            w_in, w_edge = halves(w_all[0:2 * T]), halves(w_all[2 * T:])
            x_edge = halves(dot(xp_m[...], xp[j, :, cols]))
            g_next = halves(dot(gn_m[...], gn[j, :, cols]))
            filt_f = jnp.concatenate(times_conj(g_in, x_in) + times_conj(g_edge, x_edge), axis=0)
            gfb[j, :, cols] = dot(filt_m[...], filt_f).astype(BF16)
            conv_f = jnp.concatenate(times(x_in, w_in) + times(x_edge, w_edge), axis=0)
            conv = dot(conv_m[...], conv_f)
            oq[j, :, cols] = (ob[j, :, cols].astype(F32) * conv).astype(BF16)
            grad_f = jnp.concatenate(times_conj(g_in, w_in) + times_conj(g_next, w_edge), axis=0)
            grad = dot(grad_m[...], grad_f)
            ok[j, :, cols] = (grad * vb[j, :, cols].astype(F32)).astype(BF16)
            ov[j, :, cols] = (grad * kb[j, :, cols].astype(F32)).astype(BF16)
        for copy in stores(j):
            copy.start()

    copies0, copies1, copies2, copies3, copies4 = {}, {}, {}, {}, {}

    def reduce0(n):
        copies0[n] = w_copy(gfb.at[2 * n + 1 - core], r0.at[n], s0.at[n], q0.at[n], mate)
        copies0[n].start()

    def reduce1(n):
        copies0[n].wait_recv()
        for yq in range(NY):
            cols = pl.ds(yq * T, T)
            p0[n, yq] = (gfb[2 * n + core, :, cols].astype(F32) + r0[n, :, cols].astype(F32)).astype(BF16)
        copies1[n] = []
        for d in (1, 2, 3):
            copy = w_copy(p0.at[n, y_of(d)], r1.at[n, d - 1], s1.at[n, d - 1], q1.at[n, d - 1], at(y_of(d), xi, core))
            copy.start()
            copies1[n].append(copy)

    def reduce2(n):
        for copy in copies1[n]:
            copy.wait_recv()
        total = p0[n, yi].astype(F32)
        for d in range(3):
            total = total + r1[n, d].astype(F32)
        p1[n] = total.astype(BF16)
        copies2[n] = []
        for d in (1, 2, 3):
            rows = pl.ds(pl.multiple_of(f_of(d) * taps, taps), taps)
            copy = w_copy(p1.at[n, rows, :], r2.at[n, d - 1], s2.at[n, d - 1], q2.at[n, d - 1], {"fsdp": f_of(d)})
            copy.start()
            copies2[n].append(copy)

    def reduce3(n):
        for copy in copies2[n]:
            copy.wait_recv()
        total = p1[n, own_rows, :].astype(F32)
        for d in range(3):
            total = total + r2[n, d].astype(F32)
        r3[n, xi] = total.astype(BF16)
        copies3[n] = []
        for d in (1, 2, 3):
            copy = w_copy(r3.at[n, xi], r3.at[n, xi], s3.at[n, d - 1], q3.at[n, d - 1], at(yi, x_of(d), core))
            copy.start()
            copies3[n].append(copy)

    def reduce4(n):
        for copy in copies3[n]:
            copy.wait_recv()
        total = r3[n, 0].astype(F32)
        for x in range(1, NX):
            total = total + r3[n, x].astype(F32)
        r4[n, own] = total
        copies4[n] = []
        others = [(0, 1)] + [(d, c) for d in (1, 2, 3) for c in (0, 1)]
        for i, (d, c) in enumerate(others):
            dev = at(y_of(d), xi, core if c == 0 else 1 - core)
            copy = w_copy(r4.at[n, own], r4.at[n, own], s4.at[n, i], q4.at[n, i], dev)
            copy.start()
            copies4[n].append(copy)

    def reduce5(n):
        for copy in copies4[n]:
            copy.wait_recv()
        for y in range(NY):
            for c in range(NCORE):
                gf_ref[:, pl.ds((2 * n + c) * CW + y * T, T)] = r4[n, y * NCORE + c]

    steps = (reduce1, reduce2, reduce3, reduce4, reduce5)
    for step in range(n_super + len(steps)):
        if step < n_super:
            @pl.loop(2 * step, 2 * step + 2)
            def _(j):
                chunk(j)

            reduce0(step)
        for i, stage in enumerate(steps):
            n = step - 1 - i
            if 0 <= n < n_super:
                stage(n)

    for copy in stage2 + stage3:
        copy.wait_send()
    for n in range(n_super):
        copies0[n].wait_send()
        for copy in copies1[n] + copies2[n] + copies3[n] + copies4[n]:
            copy.wait_send()

    @pl.loop(0, n_chunk)
    def _(j):
        for copy in halo(j):
            copy.wait_send()
        for copy in stores(j):
            copy.wait()


def shards(n_ctx, norm, query_gate, key_proj, value_proj, grad_out, filters, doc_bounds, continues):
    channels = query_gate.shape[2]
    n_chunk = channels // CW
    n_super = n_chunk // 2
    taps = filters.shape[0]
    forward, conv_back, grad_back = (jnp.asarray(t) for t in tables())
    vmem = pl.BlockSpec(memory_space=pltpu.VMEM)
    hbm = pl.BlockSpec(memory_space=pl.ANY)
    big = pltpu.VMEM((n_chunk, T, CW), BF16)
    dma = pltpu.SemaphoreType.DMA
    wide = jax.ShapeDtypeStruct((T, channels), BF16)
    out = pl.pallas_call(
        functools.partial(kernel, n_ctx, norm),
        out_shape=(wide, wide, wide, jax.ShapeDtypeStruct((taps, channels), F32)),
        in_specs=[vmem] * 6 + [hbm] * 4,
        out_specs=(hbm, hbm, hbm, vmem),
        scratch_shapes=[big] * 14 + [
            pltpu.VMEM((n_super, T, CW), BF16),
            pltpu.VMEM((n_super, NY, T, T), BF16),
            pltpu.VMEM((n_super, 3, T, T), BF16),
            pltpu.VMEM((n_super, T, T), BF16),
            pltpu.VMEM((n_super, 3, taps, T), BF16),
            pltpu.VMEM((n_super, taps, T), BF16),
            pltpu.VMEM((n_super, NX, taps, T), BF16),
            pltpu.VMEM((n_super, taps, T), F32),
            pltpu.VMEM((n_super, NY * NCORE, taps, T), F32),
            pltpu.VMEM((4 * T, T), BF16),
            pltpu.VMEM((4 * T, T), BF16),
            pltpu.VMEM((2 * T, T), BF16),
            pltpu.VMEM((2 * T, T), BF16),
            pltpu.VMEM((T, 4 * T), BF16),
            pltpu.VMEM((T, 4 * T), BF16),
            pltpu.VMEM((T, 4 * T), BF16),
            dma((4, n_chunk)), dma((3, n_chunk)), dma((2, n_chunk)), dma((2, n_chunk)),
            dma((3,)), dma((3,)), dma((3,)), dma((3,)), dma((4,)), dma((4,)),
            dma((n_super,)), dma((n_super,)), dma((n_super, 3)), dma((n_super, 3)),
            dma((n_super, 3)), dma((n_super, 3)), dma((n_super, 3)), dma((n_super, 3)),
            dma((n_super, 7)), dma((n_super, 7)),
        ],
        compiler_params=pltpu.CompilerParams(
            collective_id=0, has_side_effects=True, vmem_limit_bytes=48 * 1024 * 1024),
    )(doc_bounds, continues, forward, conv_back, grad_back, filters,
      key_proj[0], value_proj[0], query_gate[0], grad_out[0])
    return out[0][None], out[1][None], out[2][None], out[3]


def solution(mesh):
    n_ctx = mesh.shape["ctx"]
    norm = 1.0 / math.sqrt(mesh.shape["fsdp"] * n_ctx * T)
    wide = P("fsdp", "ctx", "tp")
    return jax.shard_map(
        functools.partial(shards, n_ctx, norm), mesh=mesh,
        in_specs=(wide, wide, wide, wide, P("fsdp", "tp"), P("fsdp", None), P("fsdp", "ctx")),
        out_specs=(wide, wide, wide, P("fsdp", "tp")), check_vma=False)
```

time: 787 us -> 75.5 us (0.10)
  other arithmetic: 323 us -> 0 us
  local copies, waits for them, and re-layouts: 240 us -> 9.33 us
  waiting for transfers between devices: 198 us -> 0 us
  Pallas kernels: 0 us -> 64.6 us
  between operations: 14.5 us -> 1.3 us
    add x17 -> x0, other arithmetic: 207 us -> none  [the longest x8 127 us: tap_block(): grad_back = grad_back + jnp.where(reaching, ahead_rows * weight_row, 0.0)]
    dynamic_update_slice x128 -> x0, local copies, waits for them, and re-layouts: 205 us -> none  [tap_block(): lax.dynamic_update_slice_in_dim(filt_grad, tap_term[None, :], tap_index, 0)]
    psum x1 -> x0, waiting for transfers between devices: 113 us -> none  [shards(): summed_all = lax.psum(filt_grad, 'ctx')]
    reduce_sum x16 -> x0, other arithmetic: 95.8 us -> none  [tap_block(): tap_term = jnp.sum(jnp.where(inside, grad_wide * earlier, 0.0), axis=0)]
    pallas_call x0 -> x1, Pallas kernels: none -> 64.6 us  [shards(): pl.pallas_call(functools.partial(kernel, n_ctx, norm), out_shape=(wide, w...]
    reduce_scatter x1 -> x0, waiting for transfers between devices: 47.3 us -> none  [shards(): lax.psum_scatter(summed_all, 'fsdp', scatter_dimension=0, tiled=True)]
    all_gather x1 -> x0, waiting for transfers between devices: 25.2 us -> none  [shards(): weights = lax.all_gather(filters, 'fsdp', axis=0, tiled=True)]
    dynamic_slice x8 -> x0, local copies, waits for them, and re-layouts: 19.3 us -> none  [tap_block(): weight_row = lax.dynamic_slice_in_dim(weights, tap_index, 1, 0)]
  transfers between devices with their start and end apart: 5 -> 0, of which waited for: 5 -> 0; matrix products, arithmetic and copies ran while one was open for 2% -> 0% of each run, Pallas kernels for 0% -> 0%
where the time goes in v1:
time: 75.5 us; the launch traced here: 75.3 us
  Pallas kernels  64.6 us (86%)
  local copies, waits for them, and re-layouts  9.33 us (12%)
  between operations  1.3 us (2%)
    pallas_call x1, Pallas kernels, shards(): pl.pallas_call(functools.partial(kernel, n_ctx, norm), out_shape=(wide, w...  64.6 us
    unnamed x16, local copies, waits for them, and re-layouts  9.33 us

profile of v1, /device:TPU:1, one launch (start us, length us, event | category | flops | bytes accessed | tf_op | source)
XLA Modules:
  0.0 75.3 jit_solution(4523399106584156432)
XLA Ops:
  1.3 0.0 copy-start.5
  1.3 0.6 copy-done.5
  1.9 0.0 copy-start
  1.9 1.2 %copy-done = bf16[1,128,4096]{2,1,0:T(8,128)(2,1)S(1)} copy-done((bf16[1,128,4096]{2,1,0:T(8,128)(2,1)S(1)}, bf16[1,128,4096]{2,1,0:T(8,128)(2,1)}, u32[]{:S(2)}) %copy-start) | copy-done | bytes 1048600
  3.2 0.0 copy-start.1
  3.2 1.0 %copy-done.1 = f32[32,4096]{1,0:T(8,128)S(1)} copy-done((f32[32,4096]{1,0:T(8,128)S(1)}, f32[32,4096]{1,0:T(8,128)}, u32[]{:S(2)}) %copy-start.1) | copy-done | bytes 524312
  4.2 0.0 copy-start.2
  4.2 0.9 %copy-done.2 = f32[128,256]{1,0:T(8,128)S(1)} copy-done((f32[128,256]{1,0:T(8,128)S(1)}, f32[128,256]{1,0:T(8,128)}, u32[]{:S(2)}) %copy-start.2) | copy-done | bytes 131096
  5.1 0.0 copy-start.3
  5.1 0.9 %copy-done.3 = f32[128,256]{1,0:T(8,128)S(1)} copy-done((f32[128,256]{1,0:T(8,128)S(1)}, f32[128,256]{1,0:T(8,128)}, u32[]{:S(2)}) %copy-start.3) | copy-done | bytes 131096
  6.0 0.0 copy-start.4
  6.0 0.9 %copy-done.4 = f32[256,128]{1,0:T(8,128)S(1)} copy-done((f32[256,128]{1,0:T(8,128)S(1)}, f32[256,128]{1,0:T(8,128)}, u32[]{:S(2)}) %copy-start.4) | copy-done | bytes 131096
  6.9 64.6 %shard_map.129 = (bf16[128,4096]{1,0:T(8,128)(2,1)S(1)}, bf16[128,4096]{1,0:T(8,128)(2,1)S(1)}, bf16[128,4096]{1,0:T(8,128)(2,1)S(1)}, f32[32,4096]{1,0:T(8,128)S(1)}) custom-call(s32[1,49]{1,0:T(1,128)S(1)} %copy-done.5, s32[1,1]{1,0:T(1,128)S(6)} %copy.18.cont_ref, f32[256,128]{1,0:T(8,128)S(1)} %copy-done.4, f32[128,256]{1,0:T(8,128)S(1)} %copy-done.3, ...), custom_call_target="tpu_custom_call" | custom-call | tf_op jit(solution)/shard_map/pallas_call | solution.py:348
  71.5 1.0 %copy.19 = bf16[1,128,4096]{2,1,0:T(8,128)(2,1)} copy(bf16[1,128,4096]{2,1,0:T(8,128)(2,1)S(1)} %bitcast.9) | data formatting | bytes 2097152
  72.5 1.0 %copy.20 = bf16[1,128,4096]{2,1,0:T(8,128)(2,1)} copy(bf16[1,128,4096]{2,1,0:T(8,128)(2,1)S(1)} %bitcast.8) | data formatting | bytes 2097152
  73.5 1.0 %copy.21 = bf16[1,128,4096]{2,1,0:T(8,128)(2,1)} copy(bf16[1,128,4096]{2,1,0:T(8,128)(2,1)S(1)} %bitcast.7) | data formatting | bytes 2097152
  74.5 0.8 %copy.22 = f32[32,4096]{1,0:T(8,128)} copy(f32[32,4096]{1,0:T(8,128)S(1)} %get-tuple-element.19) | data formatting | bytes 1048576
Async XLA Ops:
  1.3 0.7 copy-start.5
  1.9 1.2 %copy-start = (bf16[1,128,4096]{2,1,0:T(8,128)(2,1)S(1)}, bf16[1,128,4096]{2,1,0:T(8,128)(2,1)}, u32[]{:S(2)}) copy-start(bf16[1,128,4096]{2,1,0:T(8,128)(2,1)} %param.11) | copy-start | bytes 3145732
  3.2 1.0 %copy-start.1 = (f32[32,4096]{1,0:T(8,128)S(1)}, f32[32,4096]{1,0:T(8,128)}, u32[]{:S(2)}) copy-start(f32[32,4096]{1,0:T(8,128)} %filt_ref.1) | copy-start | bytes 1572868
  4.2 0.9 %copy-start.2 = (f32[128,256]{1,0:T(8,128)S(1)}, f32[128,256]{1,0:T(8,128)}, u32[]{:S(2)}) copy-start(f32[128,256]{1,0:T(8,128)} %constant.8.clone.gback_ref) | copy-start | bytes 393220
  5.1 0.9 %copy-start.3 = (f32[128,256]{1,0:T(8,128)S(1)}, f32[128,256]{1,0:T(8,128)}, u32[]{:S(2)}) copy-start(f32[128,256]{1,0:T(8,128)} %constant.7.clone.cback_ref) | copy-start | bytes 393220
  6.0 0.9 %copy-start.4 = (f32[256,128]{1,0:T(8,128)S(1)}, f32[256,128]{1,0:T(8,128)}, u32[]{:S(2)}) copy-start(f32[256,128]{1,0:T(8,128)} %constant.6.clone.fwd_ref) | copy-start | bytes 393220

commit v2 on v1

v2 whole, which is shorter than its diff:
```python
import functools
import math

import jax
import jax.numpy as jnp
from jax import lax
from jax.experimental import pallas as pl
from jax.experimental.pallas import tpu as pltpu
from jax.sharding import PartitionSpec as P

MESH = pl.DeviceIdType.MESH
T = 128
CW = 512
F32 = jnp.float32
BF16 = jnp.bfloat16
NY, NX, NCORE, NF = 4, 4, 2, 4
BIG = 1e6


def turn_cos(u):
    u = u - jnp.floor(u + 0.5)
    z = u * u
    total = None
    for n in range(8, -1, -1):
        c = (-1.0) ** n * (2 * math.pi) ** (2 * n) / math.factorial(2 * n)
        total = jnp.full_like(z, c) if total is None else total * z + c
    return total


def turn_sin(u):
    u = u - jnp.floor(u + 0.5)
    z = u * u
    total = None
    for n in range(8, -1, -1):
        c = (-1.0) ** n * (2 * math.pi) ** (2 * n + 1) / math.factorial(2 * n + 1)
        total = jnp.full_like(z, c) if total is None else total * z + c
    return total * u


def dot(a, b):
    return jnp.dot(a, b, preferred_element_type=F32)


def kernel(n_ctx, norm, bounds_hbm, cont_hbm, filt_hbm, k_hbm, v_hbm, q_hbm, o_hbm,
           gq_out, gk_out, gv_out, gf_out,
           oq, ok, ov, gf_ref, bounds_ref, cont_ref, filt_ref, kb, vb, qb, ob, xb, gb, gm, xp, gn, wb, xi_s, gi_s, filt_f,
           gfb, r0, p0, r1, p1, r2, r3, r4,
           a_m, g0_m, xt_m, xp_m, fwd_m, w_m, conv_m, grad_m, filt_m,
           small_sem, out_sem, in_sem, hs_sem, hr_sem, ws1, wr1, ws2, wr2, ws3, wr3,
           s0, q0, s1, q1, s2, q2, s3, q3, s4, q4):
    n_chunk = xb.shape[0]
    half = n_chunk // 2
    taps = T // NF
    ctx = lax.axis_index("ctx")
    fs = lax.axis_index("fsdp")
    core = lax.rem(ctx, NCORE)
    xi = lax.rem(ctx // NCORE, NX)
    yi = ctx // (NCORE * NX)
    own = yi * NCORE + core
    own_rows = pl.ds(pl.multiple_of(fs * taps, taps), taps)
    own_cols = pl.ds(pl.multiple_of(own * CW, CW), CW)

    def at(y, x, c):
        return {"ctx": (y * NX + x) * NCORE + c}

    def y_of(d):
        return lax.rem(yi + d, NY)

    def x_of(d):
        return lax.rem(xi + d, NX)

    def f_of(d):
        return lax.rem(fs + d, NF)

    def send(src, dst, s, r, dev):
        return pltpu.make_async_remote_copy(src_ref=src, dst_ref=dst, send_sem=s, recv_sem=r,
                                            device_id=dev, device_id_type=MESH)

    nxt = {"ctx": lax.rem(ctx + 1, n_ctx)}
    prv = {"ctx": lax.rem(ctx + n_ctx - 1, n_ctx)}
    mate = at(yi, xi, 1 - core)
    peers = [nxt, prv, mate]
    peers += [{"fsdp": f_of(d)} for d in (1, 2, 3)]
    peers += [at(y_of(d), xi, c) for d in (1, 2, 3) for c in (core, 1 - core)]
    peers += [at(yi, x_of(d), core) for d in (1, 2, 3)]
    barrier = pltpu.get_barrier_semaphore()
    for peer in peers:
        pl.semaphore_signal(barrier, inc=1, device_id=peer, device_id_type=MESH)

    small = [pltpu.make_async_copy(bounds_hbm, bounds_ref, small_sem.at[0]),
             pltpu.make_async_copy(cont_hbm, cont_ref, small_sem.at[1]),
             pltpu.make_async_copy(filt_hbm.at[:, own_cols], filt_ref, small_sem.at[2])]
    for copy in small:
        copy.start()

    def loads(j):
        cols = pl.ds(pl.multiple_of(j * CW, CW), CW)
        return [pltpu.make_async_copy(src.at[:, cols], dst.at[j], in_sem.at[i, j])
                for i, (src, dst) in enumerate(((k_hbm, kb), (v_hbm, vb), (q_hbm, qb), (o_hbm, ob)))]

    @pl.loop(0, n_chunk)
    def _(j):
        for copy in loads(j):
            copy.start()

    for copy in small:
        copy.wait()
    wb[own, own_rows, :] = filt_ref[...].astype(BF16)

    first = (ctx * T).astype(F32)
    bounds = bounds_ref[...].astype(F32)
    flag = cont_ref[...] == 1
    row = lax.broadcasted_iota(jnp.int32, (T, 1), 0).astype(F32)
    lane = lax.broadcasted_iota(jnp.int32, (1, T), 1).astype(F32)
    first_cut = jnp.min(jnp.where(bounds >= first, bounds, BIG), axis=1, keepdims=True) - first
    head_row = jnp.logical_and(row < first_cut, flag)
    head_lane = jnp.logical_and(lane < first_cut, flag)

    @pl.loop(0, n_chunk)
    def _(j):
        for copy in loads(j):
            copy.wait()
        xb[j] = (kb[j].astype(F32) * vb[j].astype(F32)).astype(BF16)
        grad_conv = (ob[j].astype(F32) * qb[j].astype(F32)).astype(BF16)
        gb[j] = grad_conv
        gm[j] = jnp.where(head_row, grad_conv.astype(F32), 0.0).astype(BF16)

    low = jnp.max(jnp.where(bounds <= row + first, bounds, 0.0), axis=1, keepdims=True)
    high = jnp.min(jnp.where(bounds > row + first, bounds, BIG), axis=1, keepdims=True)
    begin = jnp.maximum(low - first, 0.0)
    end = jnp.minimum(high - first, float(T))
    size = end - begin
    prev_start = jnp.max(jnp.where(bounds <= first, bounds, 0.0), axis=1, keepdims=True) - first + T
    last_start = jnp.max(jnp.where(bounds <= first + (T - 1), bounds, 0.0), axis=1, keepdims=True) - first

    freq = (row - begin + 0.5) / (2.0 * size)
    same = jnp.logical_and(lane >= begin, lane < end)
    turn = freq * (lane - begin)
    a_re = jnp.where(same, turn_cos(turn), 0.0)
    a_im = jnp.where(same, -turn_sin(turn), 0.0)
    short = lane < size
    turn = freq * lane
    b_re = jnp.where(short, turn_cos(turn), 0.0) / size
    b_im = jnp.where(short, -turn_sin(turn), 0.0) / size
    turn = (row + 0.5) * lane * (0.5 / T)
    for i, part in enumerate((turn_cos(turn), -turn_sin(turn))):
        rows = pl.ds(i * T, T)
        fwd_m[rows, :] = part.astype(BF16)
        w_m[pl.ds((2 + i) * T, T), :] = part.astype(BF16)
        g0_m[rows, :] = jnp.where(head_lane, part, 0.0).astype(BF16)
        xt_m[rows, :] = jnp.where(lane >= last_start, part, 0.0).astype(BF16)
        xp_m[rows, :] = jnp.where(lane >= prev_start, part, 0.0).astype(BF16)
    for i, (a, b) in enumerate(((a_re, b_re), (a_im, b_im))):
        rows = pl.ds(i * T, T)
        a_m[rows, :] = a.astype(BF16)
        w_m[rows, :] = b.astype(BF16)
        a_back = a.T.astype(BF16)
        conv_m[:, rows] = a_back
        grad_m[:, rows] = a_back
        filt_m[:, rows] = (b * norm).T.astype(BF16)
    turn = (lane + 0.5) * (row + T) * (0.5 / T)
    for i, part in enumerate((turn_cos(turn), -turn_sin(turn))):
        conv_m[:, pl.ds((2 + i) * T, T)] = jnp.where(head_row, part / T, 0.0).astype(BF16)
    turn = (lane + 0.5) * (row - T) * (0.5 / T)
    for i, part in enumerate((turn_cos(turn), -turn_sin(turn))):
        cols = pl.ds((2 + i) * T, T)
        grad_m[:, cols] = jnp.where(row >= last_start, part / T, 0.0).astype(BF16)
        filt_m[:, cols] = (part * (norm / T)).astype(BF16)

    pl.semaphore_wait(barrier, len(peers))

    stage1 = [send(wb.at[own, own_rows, :], wb.at[own, own_rows, :], ws1.at[d - 1], wr1.at[d - 1], {"fsdp": f_of(d)})
              for d in (1, 2, 3)]
    for copy in stage1:
        copy.start()

    def rows_on(j):
        return send(xb.at[j], xp.at[j], hs_sem.at[0, j], hr_sem.at[0, j], nxt)

    def rows_back(j):
        return send(gm.at[j], gn.at[j], hs_sem.at[1, j], hr_sem.at[1, j], prv)

    @pl.loop(0, half)
    def _(i):
        rows_on(i).start()
        rows_back(half + i).start()

    def times(a, b):
        return [(a[0] * b[0] - a[1] * b[1]).astype(BF16), (a[0] * b[1] + a[1] * b[0]).astype(BF16)]

    def times_conj(a, b):
        return [(a[0] * b[0] + a[1] * b[1]).astype(BF16), (a[1] * b[0] - a[0] * b[1]).astype(BF16)]

    def halves(a):
        return [a[0:T], a[T:2 * T]]

    def put(ref, j, start, cols, parts):
        for i, part in enumerate(parts):
            ref[j, pl.ds(start + i * T, T), cols] = part

    blocks = [pl.ds(c, 256) for c in range(0, CW, 256)]

    @pl.loop(0, n_chunk)
    def _(j):
        for cols in blocks:
            x_in = dot(a_m[...], xb[j, :, cols])
            g_in = dot(a_m[...], gb[j, :, cols])
            xi_s[j, :, cols] = x_in
            gi_s[j, :, cols] = g_in
            put(filt_f, j, 0, cols, times_conj(halves(g_in), halves(x_in)))

    for copy in stage1:
        copy.wait()
    stage2 = [send(wb.at[own], wb.at[own], ws2.at[d - 1], wr2.at[d - 1], at(y_of(d), xi, core)) for d in (1, 2, 3)]
    for copy in stage2:
        copy.start()
    stage3 = [send(wb.at[own], wb.at[own], ws3.at[0], wr3.at[0], mate)]
    stage3[0].start()

    def filt_grad(j, wave, side, g_m, g_ref, x_m, x_ref):
        for c, cols in enumerate(blocks):
            g_edge = halves(dot(g_m[...], g_ref[j, :, cols]))
            x_edge = halves(dot(x_m[...], x_ref[j, :, cols]))
            put(filt_f, j, 2 * T, cols, times_conj(g_edge, x_edge))
            gfb[wave, lax.rem(j, NCORE), :, pl.ds(side * CW + c * 256, 256)] = dot(
                filt_m[...], filt_f[j, :, cols]).astype(BF16)

    def wave_work(wave):
        @pl.loop(2 * wave, 2 * wave + 2)
        def _(i):
            rows_on(i).wait_recv()
            rows_on(half + i).start()
            filt_grad(i, wave, 0, g0_m, gb, xp_m, xp)
            rows_back(half + i).wait_recv()
            rows_back(i).start()
            filt_grad(half + i, wave, 1, fwd_m, gn, xt_m, xb)

    sent0, sent1, sent2, sent3, sent4 = {}, {}, {}, {}, {}

    def reduce0(n):
        sent0[n] = [send(gfb.at[n, 1 - core], r0.at[n], s0.at[n], q0.at[n], mate)]
        for copy in sent0[n]:
            copy.start()

    def reduce1(n):
        for copy in sent0[n]:
            copy.wait_recv()
        for yq in range(NY):
            for side in range(2):
                cols = pl.ds(side * CW + yq * T, T)
                p0[n, yq, :, pl.ds(side * T, T)] = (
                    gfb[n, core, :, cols].astype(F32) + r0[n, :, cols].astype(F32)).astype(BF16)
        sent1[n] = [send(p0.at[n, y_of(d)], r1.at[n, d - 1], s1.at[n, d - 1], q1.at[n, d - 1], at(y_of(d), xi, core))
                    for d in (1, 2, 3)]
        for copy in sent1[n]:
            copy.start()

    def reduce2(n):
        for copy in sent1[n]:
            copy.wait_recv()
        total = p0[n, yi].astype(F32)
        for d in range(3):
            total = total + r1[n, d].astype(F32)
        p1[n] = total.astype(BF16)
        sent2[n] = [send(p1.at[n, pl.ds(pl.multiple_of(f_of(d) * taps, taps), taps), :], r2.at[n, d - 1],
                         s2.at[n, d - 1], q2.at[n, d - 1], {"fsdp": f_of(d)}) for d in (1, 2, 3)]
        for copy in sent2[n]:
            copy.start()

    def reduce3(n):
        for copy in sent2[n]:
            copy.wait_recv()
        total = p1[n, own_rows, :].astype(F32)
        for d in range(3):
            total = total + r2[n, d].astype(F32)
        r3[n, xi] = total.astype(BF16)
        sent3[n] = [send(r3.at[n, xi], r3.at[n, xi], s3.at[n, d - 1], q3.at[n, d - 1], at(yi, x_of(d), core))
                    for d in (1, 2, 3)]
        for copy in sent3[n]:
            copy.start()

    def reduce4(n):
        for copy in sent3[n]:
            copy.wait_recv()
        total = r3[n, 0].astype(F32)
        for x in range(1, NX):
            total = total + r3[n, x].astype(F32)
        r4[n, own] = total.astype(BF16)
        others = [(0, 1 - core)] + [(d, c) for d in (1, 2, 3) for c in (core, 1 - core)]
        sent4[n] = [send(r4.at[n, own], r4.at[n, own], s4.at[n, i], q4.at[n, i], at(y_of(d), xi, c))
                    for i, (d, c) in enumerate(others)]
        for copy in sent4[n]:
            copy.start()

    def reduce5(n):
        for copy in sent4[n]:
            copy.wait_recv()
        for y in range(NY):
            for c in range(NCORE):
                for side in range(2):
                    gf_ref[:, pl.ds((side * half + 2 * n + c) * CW + y * T, T)] = (
                        r4[n, y * NCORE + c, :, pl.ds(side * T, T)].astype(F32))

    def conv_and_grad(start, stop):
        @pl.loop(start, stop)
        def _(j):
            for cols in blocks:
                x_in, g_in = halves(xi_s[j, :, cols]), halves(gi_s[j, :, cols])
                w_all = dot(w_m[...], wb[j, :, cols])
                w_in, w_edge = halves(w_all[0:2 * T]), halves(w_all[2 * T:])
                x_edge = halves(dot(xp_m[...], xp[j, :, cols]))
                g_next = halves(dot(fwd_m[...], gn[j, :, cols]))
                conv_f = jnp.concatenate(times(x_in, w_in) + times(x_edge, w_edge), axis=0)
                conv = dot(conv_m[...], conv_f)
                oq[j, :, cols] = (ob[j, :, cols].astype(F32) * conv).astype(BF16)
                grad_f = jnp.concatenate(times_conj(g_in, w_in) + times_conj(g_next, w_edge), axis=0)
                grad = dot(grad_m[...], grad_f)
                ok[j, :, cols] = (grad * vb[j, :, cols].astype(F32)).astype(BF16)
                ov[j, :, cols] = (grad * kb[j, :, cols].astype(F32)).astype(BF16)
            for copy in stores(j):
                copy.start()

    def stores(j):
        cols = pl.ds(pl.multiple_of(j * CW, CW), CW)
        return [pltpu.make_async_copy(src.at[j], dst.at[:, cols], out_sem.at[i, j])
                for i, (src, dst) in enumerate(((oq, gq_out), (ok, gk_out), (ov, gv_out)))]

    wave_work(0)
    reduce0(0)
    wave_work(1)
    reduce0(1)
    reduce1(0)
    reduce1(1)
    for d in (1, 2, 3):
        stage2[d - 1].wait_recv()
        got = lax.rem(yi + NY - d, NY) * NCORE + core
        stage3.append(send(wb.at[got], wb.at[got], ws3.at[d], wr3.at[d], mate))
        stage3[d].start()
    reduce2(0)
    for copy in stage3:
        copy.wait_recv()

    @pl.loop(0, half)
    def _(i):
        rows_on(half + i).wait_recv()
        rows_back(i).wait_recv()

    conv_and_grad(0, 2)
    reduce2(1)
    reduce3(0)
    conv_and_grad(2, 5)
    reduce3(1)
    reduce4(0)
    conv_and_grad(5, n_chunk)
    reduce4(1)
    reduce5(0)
    reduce5(1)
    last = pltpu.make_async_copy(gf_ref, gf_out, small_sem.at[0])
    last.start()

    for copy in stage2 + stage3:
        copy.wait_send()
    for n in range(2):
        for copy in sent0[n] + sent1[n] + sent2[n] + sent3[n] + sent4[n]:
            copy.wait_send()

    @pl.loop(0, n_chunk)
    def _(j):
        rows_on(j).wait_send()
        rows_back(j).wait_send()
        for copy in stores(j):
            copy.wait()

    last.wait()


def write_out(a, b, c, d, a_hbm, b_hbm, c_hbm, d_hbm, va, vb, vc, vd, in_sem, out_sem):
    parts = []
    for i, (src, mid, dst) in enumerate(((a, va, a_hbm), (b, vb, b_hbm), (c, vc, c_hbm), (d, vd, d_hbm))):
        step = src.shape[0] // 2
        for h in range(2):
            rows = pl.ds(h * step, step)
            parts.append((pltpu.make_async_copy(src.at[rows], mid.at[rows], in_sem.at[i, h]),
                          pltpu.make_async_copy(mid.at[rows], dst.at[rows], out_sem.at[i, h])))
    for get, _ in parts:
        get.start()
    for get, put in parts:
        get.wait()
        put.start()
    for _, put in parts:
        put.wait()


def shards(n_ctx, norm, query_gate, key_proj, value_proj, grad_out, filters, doc_bounds, continues):
    channels = query_gate.shape[2]
    n_chunk = channels // CW
    taps = filters.shape[0]
    hbm = pl.BlockSpec(memory_space=pl.ANY)
    pinned = pl.BlockSpec(memory_space=pltpu.HBM)
    dma = pltpu.SemaphoreType.DMA
    wide = jax.ShapeDtypeStruct((T, channels), BF16)
    shapes = (wide, wide, wide, jax.ShapeDtypeStruct((taps, channels), F32))

    def chunks(rows, dtype):
        return pltpu.VMEM((n_chunk, rows, CW), dtype)

    mine = pl.pallas_call(
        functools.partial(kernel, n_ctx, norm),
        out_shape=shapes,
        in_specs=[pinned] * 7,
        out_specs=(hbm,) * 4,
        scratch_shapes=[chunks(T, BF16)] * 3 + [pltpu.VMEM((taps, channels), F32)] + [pltpu.VMEM(doc_bounds.shape, jnp.int32), pltpu.VMEM((1, 1), jnp.int32), pltpu.VMEM((taps, CW), F32)]
        + [chunks(T, BF16)] * 10 + [chunks(2 * T, F32)] * 2 + [chunks(4 * T, BF16)] + [
            pltpu.VMEM((2, NCORE, T, 2 * CW), BF16),
            pltpu.VMEM((2, T, 2 * CW), BF16),
            pltpu.VMEM((2, NY, T, 2 * T), BF16),
            pltpu.VMEM((2, 3, T, 2 * T), BF16),
            pltpu.VMEM((2, T, 2 * T), BF16),
            pltpu.VMEM((2, 3, taps, 2 * T), BF16),
            pltpu.VMEM((2, NX, taps, 2 * T), BF16),
            pltpu.VMEM((2, NY * NCORE, taps, 2 * T), BF16),
        ] + [pltpu.VMEM((2 * T, T), BF16)] * 5 + [pltpu.VMEM((4 * T, T), BF16)] + [pltpu.VMEM((T, 4 * T), BF16)] * 3 + [
            dma((3,)), dma((3, n_chunk)), dma((4, n_chunk)), dma((2, n_chunk)), dma((2, n_chunk)),
            dma((3,)), dma((3,)), dma((3,)), dma((3,)), dma((4,)), dma((4,)),
            dma((2,)), dma((2,)), dma((2, 3)), dma((2, 3)), dma((2, 3)), dma((2, 3)), dma((2, 3)), dma((2, 3)),
            dma((2, 7)), dma((2, 7)),
        ],
        compiler_params=pltpu.CompilerParams(
            collective_id=0, has_side_effects=True, vmem_limit_bytes=62 * 1024 * 1024),
    )(doc_bounds, continues, filters, key_proj[0], value_proj[0], query_gate[0], grad_out[0])
    out = pl.pallas_call(
        write_out, out_shape=shapes, in_specs=[hbm] * 4, out_specs=(pinned,) * 4, scratch_shapes=[pltpu.VMEM(t.shape, t.dtype) for t in shapes] + [dma((4, 2)), dma((4, 2))],
        compiler_params=pltpu.CompilerParams(vmem_limit_bytes=62 * 1024 * 1024),
    )(*mine)
    return out[0][None], out[1][None], out[2][None], out[3]


def solution(mesh):
    n_ctx = mesh.shape["ctx"]
    norm = 1.0 / math.sqrt(mesh.shape["fsdp"] * n_ctx * T)
    wide = P("fsdp", "ctx", "tp")
    return jax.shard_map(
        functools.partial(shards, n_ctx, norm), mesh=mesh,
        in_specs=(wide, wide, wide, wide, P("fsdp", "tp"), P("fsdp", None), P("fsdp", "ctx")),
        out_specs=(wide, wide, wide, P("fsdp", "tp")), check_vma=False)
```

time: 75.5 us -> 55.8 us (0.74)
  Pallas kernels: 64.6 us -> 54.4 us
  local copies, waits for them, and re-layouts: 9.33 us -> 0 us
    pallas_call x1 -> x2, Pallas kernels: 64.6 us -> 54.4 us  [the longest x1 51.4 us: shards(): pl.pallas_call(functools.partial(kernel, n_ctx, norm), out_shape=shapes,...]
    unnamed x16 -> x0, local copies, waits for them, and re-layouts: 9.33 us -> none
where the time goes in v2:
time: 55.8 us; the launch traced here: 55.7 us
  Pallas kernels  54.4 us (97%)
  between operations  1.29 us (2%)
    pallas_call x1, Pallas kernels, shards(): pl.pallas_call(functools.partial(kernel, n_ctx, norm), out_shape=shapes,...  51.4 us
    pallas_call x1, Pallas kernels, shards(): pl.pallas_call(write_out, out_shape=shapes, in_specs=[hbm] * 4, out_specs...  3.01 us

profile of v2, /device:TPU:1, one launch (start us, length us, event | category | flops | bytes accessed | tf_op | source)
XLA Modules:
  0.0 55.7 jit_solution(12147427200731883641)
XLA Ops:
  1.3 51.4 %shard_map.102 = (bf16[128,4096]{1,0:T(8,128)(2,1)}, bf16[128,4096]{1,0:T(8,128)(2,1)}, bf16[128,4096]{1,0:T(8,128)(2,1)}, f32[32,4096]{1,0:T(8,128)}) custom-call(s32[1,49]{1,0:T(1,128)} %bounds_hbm.1, s32[1,1]{1,0:T(1,128)S(6)} %copy.11.cont_hbm, f32[32,4096]{1,0:T(8,128)} %filt_hbm.1, bf16[128,4096]{1,0:T(8,128)(2,1)} %bitcast.7, ...), custom_call_target="tpu_custom_call" | custom-call | tf_op jit(solution)/shard_map/pallas_call | solution.py:407
  52.7 3.0 %shard_map.103 = (bf16[128,4096]{1,0:T(8,128)(2,1)}, bf16[128,4096]{1,0:T(8,128)(2,1)}, bf16[128,4096]{1,0:T(8,128)(2,1)}, f32[32,4096]{1,0:T(8,128)}) custom-call(bf16[128,4096]{1,0:T(8,128)(2,1)} %get-tuple-element.12.a, bf16[128,4096]{1,0:T(8,128)(2,1)} %get-tuple-element.13.b, bf16[128,4096]{1,0:T(8,128)(2,1)} %get-tuple-element.14.c, ...), custom_call_target="tpu_custom_call" | custom-call | tf_op jit(solution)/shard_map/pallas_call | solution.py:431

commit v3 on v2

--- a/solution.py
+++ b/solution.py
@@ -42,13 +42,13 @@
 
 
 def kernel(n_ctx, norm, bounds_hbm, cont_hbm, filt_hbm, k_hbm, v_hbm, q_hbm, o_hbm,
-           gq_out, gk_out, gv_out, gf_out,
-           oq, ok, ov, gf_ref, bounds_ref, cont_ref, filt_ref, kb, vb, qb, ob, xb, gb, gm, xp, gn, wb, xi_s, gi_s, filt_f,
+           oq, ok, ov, gf_ref,
+           bounds_ref, cont_ref, filt_ref, kb, vb, qb, ob, gb, edge_out, edge_in, wb, xi_s, gi_s, filt_f,
            gfb, r0, p0, r1, p1, r2, r3, r4,
            a_m, g0_m, xt_m, xp_m, fwd_m, w_m, conv_m, grad_m, filt_m,
-           small_sem, out_sem, in_sem, hs_sem, hr_sem, ws1, wr1, ws2, wr2, ws3, wr3,
+           small_sem, in_sem, hs_sem, hr_sem, ws1, wr1, ws2, wr2,
            s0, q0, s1, q1, s2, q2, s3, q3, s4, q4):
-    n_chunk = xb.shape[0]
+    n_chunk = gb.shape[0]
     half = n_chunk // 2
     taps = T // NF
     ctx = lax.axis_index("ctx")
@@ -57,8 +57,9 @@
     xi = lax.rem(ctx // NCORE, NX)
     yi = ctx // (NCORE * NX)
     own = yi * NCORE + core
+    own_half = pl.ds(core * half, half)
     own_rows = pl.ds(pl.multiple_of(fs * taps, taps), taps)
-    own_cols = pl.ds(pl.multiple_of(own * CW, CW), CW)
+    own_cols = pl.ds(pl.multiple_of(core * half * CW, half * CW), half * CW)
 
     def at(y, x, c):
         return {"ctx": (y * NX + x) * NCORE + c}
@@ -105,7 +106,8 @@
 
     for copy in small:
         copy.wait()
-    wb[own, own_rows, :] = filt_ref[...].astype(BF16)
+    for i in range(half):
+        wb[core * half + i, own_rows, :] = filt_ref[:, i * CW:(i + 1) * CW].astype(BF16)
 
     first = (ctx * T).astype(F32)
     bounds = bounds_ref[...].astype(F32)
@@ -120,10 +122,10 @@
     def _(j):
         for copy in loads(j):
             copy.wait()
-        xb[j] = (kb[j].astype(F32) * vb[j].astype(F32)).astype(BF16)
+        edge_out[0, j] = (kb[j].astype(F32) * vb[j].astype(F32)).astype(BF16)
         grad_conv = (ob[j].astype(F32) * qb[j].astype(F32)).astype(BF16)
         gb[j] = grad_conv
-        gm[j] = jnp.where(head_row, grad_conv.astype(F32), 0.0).astype(BF16)
+        edge_out[1, j] = jnp.where(head_row, grad_conv.astype(F32), 0.0).astype(BF16)
 
     low = jnp.max(jnp.where(bounds <= row + first, bounds, 0.0), axis=1, keepdims=True)
     high = jnp.min(jnp.where(bounds > row + first, bounds, BIG), axis=1, keepdims=True)
@@ -167,24 +169,6 @@
         grad_m[:, cols] = jnp.where(row >= last_start, part / T, 0.0).astype(BF16)
         filt_m[:, cols] = (part * (norm / T)).astype(BF16)
 
-    pl.semaphore_wait(barrier, len(peers))
-
-    stage1 = [send(wb.at[own, own_rows, :], wb.at[own, own_rows, :], ws1.at[d - 1], wr1.at[d - 1], {"fsdp": f_of(d)})
-              for d in (1, 2, 3)]
-    for copy in stage1:
-        copy.start()
-
-    def rows_on(j):
-        return send(xb.at[j], xp.at[j], hs_sem.at[0, j], hr_sem.at[0, j], nxt)
-
-    def rows_back(j):
-        return send(gm.at[j], gn.at[j], hs_sem.at[1, j], hr_sem.at[1, j], prv)
-
-    @pl.loop(0, half)
-    def _(i):
-        rows_on(i).start()
-        rows_back(half + i).start()
-
     def times(a, b):
         return [(a[0] * b[0] - a[1] * b[1]).astype(BF16), (a[0] * b[1] + a[1] * b[0]).astype(BF16)]
 
@@ -203,37 +187,57 @@
     @pl.loop(0, n_chunk)
     def _(j):
         for cols in blocks:
-            x_in = dot(a_m[...], xb[j, :, cols])
+            x_in = dot(a_m[...], edge_out[0, j, :, cols])
             g_in = dot(a_m[...], gb[j, :, cols])
             xi_s[j, :, cols] = x_in
             gi_s[j, :, cols] = g_in
             put(filt_f, j, 0, cols, times_conj(halves(g_in), halves(x_in)))
 
-    for copy in stage1:
-        copy.wait()
-    stage2 = [send(wb.at[own], wb.at[own], ws2.at[d - 1], wr2.at[d - 1], at(y_of(d), xi, core)) for d in (1, 2, 3)]
-    for copy in stage2:
+    pl.semaphore_wait(barrier, len(peers))
+
+    wide_rows = wb.at[own_half, own_rows, :]
+    stage1 = [send(wide_rows, wide_rows, ws1.at[d - 1], wr1.at[d - 1], {"fsdp": f_of(d)}) for d in (1, 2, 3)]
+    stage2 = [send(wide_rows, wide_rows, ws2.at[0], wr2.at[0], mate)]
+    for copy in stage1 + stage2:
         copy.start()
-    stage3 = [send(wb.at[own], wb.at[own], ws3.at[0], wr3.at[0], mate)]
-    stage3[0].start()
-
-    def filt_grad(j, wave, side, g_m, g_ref, x_m, x_ref):
+
+    def edge(way, j):
+        return send(edge_out.at[way, j], edge_in.at[way, j], hs_sem.at[way, j], hr_sem.at[way, j],
+                    {"ctx": lax.rem(ctx + 1 - 2 * way + n_ctx, n_ctx)})
+
+    def early(way, i):
+        return edge(way, way * half + i)
+
+    def late(way, i):
+        return edge(way, (1 - way) * half + i)
+
+    for part in (early, late):
+        for way in (1 - core, core):
+            @pl.loop(0, half)
+            def _(i):
+                part(way, i).start()
+
+
+    def share_filters():
+        for d in (1, 2, 3):
+            stage1[d - 1].wait_recv()
+            got = wb.at[own_half, pl.ds(pl.multiple_of(lax.rem(fs + NF - d, NF) * taps, taps), taps), :]
+            stage2.append(send(got, got, ws2.at[d], wr2.at[d], mate))
+            stage2[d].start()
+
+    def filt_grad(wave, side, g_m, g_rows, x_m, x_rows):
+        j = side * half + wave
         for c, cols in enumerate(blocks):
-            g_edge = halves(dot(g_m[...], g_ref[j, :, cols]))
-            x_edge = halves(dot(x_m[...], x_ref[j, :, cols]))
+            g_edge = halves(dot(g_m[...], g_rows[:, cols]))
+            x_edge = halves(dot(x_m[...], x_rows[:, cols]))
             put(filt_f, j, 2 * T, cols, times_conj(g_edge, x_edge))
-            gfb[wave, lax.rem(j, NCORE), :, pl.ds(side * CW + c * 256, 256)] = dot(
-                filt_m[...], filt_f[j, :, cols]).astype(BF16)
+            gfb[wave, side, :, cols] = dot(filt_m[...], filt_f[j, :, cols]).astype(BF16)
 
     def wave_work(wave):
-        @pl.loop(2 * wave, 2 * wave + 2)
-        def _(i):
-            rows_on(i).wait_recv()
-            rows_on(half + i).start()
-            filt_grad(i, wave, 0, g0_m, gb, xp_m, xp)
-            rows_back(half + i).wait_recv()
-            rows_back(i).start()
-            filt_grad(half + i, wave, 1, fwd_m, gn, xt_m, xb)
+        early(0, wave).wait_recv()
+        filt_grad(wave, 0, g0_m, gb.at[wave], xp_m, edge_in.at[0, wave])
+        early(1, wave).wait_recv()
+        filt_grad(wave, 1, fwd_m, edge_in.at[1, half + wave], xt_m, edge_out.at[0, half + wave])
 
     sent0, sent1, sent2, sent3, sent4 = {}, {}, {}, {}, {}
 
@@ -246,10 +250,8 @@
         for copy in sent0[n]:
             copy.wait_recv()
         for yq in range(NY):
-            for side in range(2):
-                cols = pl.ds(side * CW + yq * T, T)
-                p0[n, yq, :, pl.ds(side * T, T)] = (
-                    gfb[n, core, :, cols].astype(F32) + r0[n, :, cols].astype(F32)).astype(BF16)
+            cols = pl.ds(yq * T, T)
+            p0[n, yq] = (gfb[n, core, :, cols].astype(F32) + r0[n, :, cols].astype(F32)).astype(BF16)
         sent1[n] = [send(p0.at[n, y_of(d)], r1.at[n, d - 1], s1.at[n, d - 1], q1.at[n, d - 1], at(y_of(d), xi, core))
                     for d in (1, 2, 3)]
         for copy in sent1[n]:
@@ -297,9 +299,7 @@
             copy.wait_recv()
         for y in range(NY):
             for c in range(NCORE):
-                for side in range(2):
-                    gf_ref[:, pl.ds((side * half + 2 * n + c) * CW + y * T, T)] = (
-                        r4[n, y * NCORE + c, :, pl.ds(side * T, T)].astype(F32))
+                gf_ref[:, pl.ds((c * half + n) * CW + y * T, T)] = r4[n, y * NCORE + c].astype(F32)
 
     def conv_and_grad(start, stop):
         @pl.loop(start, stop)
@@ -308,92 +308,88 @@
                 x_in, g_in = halves(xi_s[j, :, cols]), halves(gi_s[j, :, cols])
                 w_all = dot(w_m[...], wb[j, :, cols])
                 w_in, w_edge = halves(w_all[0:2 * T]), halves(w_all[2 * T:])
-                x_edge = halves(dot(xp_m[...], xp[j, :, cols]))
-                g_next = halves(dot(fwd_m[...], gn[j, :, cols]))
+                x_edge = halves(dot(xp_m[...], edge_in[0, j, :, cols]))
+                g_next = halves(dot(fwd_m[...], edge_in[1, j, :, cols]))
                 conv_f = jnp.concatenate(times(x_in, w_in) + times(x_edge, w_edge), axis=0)
                 conv = dot(conv_m[...], conv_f)
-                oq[j, :, cols] = (ob[j, :, cols].astype(F32) * conv).astype(BF16)
+                out = pl.ds(pl.multiple_of(j * CW + cols.start, 256), 256)
+                oq[:, out] = (ob[j, :, cols].astype(F32) * conv).astype(BF16)
                 grad_f = jnp.concatenate(times_conj(g_in, w_in) + times_conj(g_next, w_edge), axis=0)
                 grad = dot(grad_m[...], grad_f)
-                ok[j, :, cols] = (grad * vb[j, :, cols].astype(F32)).astype(BF16)
-                ov[j, :, cols] = (grad * kb[j, :, cols].astype(F32)).astype(BF16)
-            for copy in stores(j):
-                copy.start()
-
-    def stores(j):
-        cols = pl.ds(pl.multiple_of(j * CW, CW), CW)
-        return [pltpu.make_async_copy(src.at[j], dst.at[:, cols], out_sem.at[i, j])
-                for i, (src, dst) in enumerate(((oq, gq_out), (ok, gk_out), (ov, gv_out)))]
+                ok[:, out] = (grad * vb[j, :, cols].astype(F32)).astype(BF16)
+                ov[:, out] = (grad * kb[j, :, cols].astype(F32)).astype(BF16)
 
     wave_work(0)
     reduce0(0)
     wave_work(1)
     reduce0(1)
     reduce1(0)
+    wave_work(2)
+    reduce0(2)
     reduce1(1)
-    for d in (1, 2, 3):
-        stage2[d - 1].wait_recv()
-        got = lax.rem(yi + NY - d, NY) * NCORE + core
-        stage3.append(send(wb.at[got], wb.at[got], ws3.at[d], wr3.at[d], mate))
-        stage3[d].start()
+    wave_work(3)
+    reduce0(3)
+    reduce1(2)
+    reduce1(3)
     reduce2(0)
-    for copy in stage3:
+    reduce2(1)
+    reduce2(2)
+    reduce2(3)
+    share_filters()
+    for copy in stage2:
         copy.wait_recv()
 
     @pl.loop(0, half)
     def _(i):
-        rows_on(half + i).wait_recv()
-        rows_back(i).wait_recv()
+        late(0, i).wait_recv()
+        late(1, i).wait_recv()
 
     conv_and_grad(0, 2)
-    reduce2(1)
     reduce3(0)
-    conv_and_grad(2, 5)
     reduce3(1)
+    conv_and_grad(2, 4)
+    reduce3(2)
+    reduce3(3)
     reduce4(0)
-    conv_and_grad(5, n_chunk)
     reduce4(1)
+    conv_and_grad(4, 6)
+    reduce4(2)
+    reduce4(3)
+    conv_and_grad(6, 8)
     reduce5(0)
     reduce5(1)
-    last = pltpu.make_async_copy(gf_ref, gf_out, small_sem.at[0])
-    last.start()
-
-    for copy in stage2 + stage3:
+    reduce5(2)
+    reduce5(3)
+
+    for copy in stage1 + stage2:
         copy.wait_send()
-    for n in range(2):
+    for n in range(half):
         for copy in sent0[n] + sent1[n] + sent2[n] + sent3[n] + sent4[n]:
             copy.wait_send()
 
     @pl.loop(0, n_chunk)
     def _(j):
-        rows_on(j).wait_send()
-        rows_back(j).wait_send()
-        for copy in stores(j):
-            copy.wait()
-
-    last.wait()
-
-
-def write_out(a, b, c, d, a_hbm, b_hbm, c_hbm, d_hbm, va, vb, vc, vd, in_sem, out_sem):
+        edge(0, j).wait_send()
+        edge(1, j).wait_send()
+
+
+def write_out(a, b, c, d, a_hbm, b_hbm, c_hbm, d_hbm, sem):
     parts = []
-    for i, (src, mid, dst) in enumerate(((a, va, a_hbm), (b, vb, b_hbm), (c, vc, c_hbm), (d, vd, d_hbm))):
+    for i, (src, dst) in enumerate(((a, a_hbm), (b, b_hbm), (c, c_hbm), (d, d_hbm))):
         step = src.shape[0] // 2
         for h in range(2):
             rows = pl.ds(h * step, step)
-            parts.append((pltpu.make_async_copy(src.at[rows], mid.at[rows], in_sem.at[i, h]),
-                          pltpu.make_async_copy(mid.at[rows], dst.at[rows], out_sem.at[i, h])))
-    for get, _ in parts:
-        get.start()
-    for get, put in parts:
-        get.wait()
+            parts.append(pltpu.make_async_copy(src.at[rows], dst.at[rows], sem.at[i, h]))
+    for put in parts:
         put.start()
-    for _, put in parts:
+    for put in parts:
         put.wait()
 
 
 def shards(n_ctx, norm, query_gate, key_proj, value_proj, grad_out, filters, doc_bounds, continues):
     channels = query_gate.shape[2]
     n_chunk = channels // CW
+    half = n_chunk // 2
     taps = filters.shape[0]
     hbm = pl.BlockSpec(memory_space=pl.ANY)
     pinned = pl.BlockSpec(memory_space=pltpu.HBM)
@@ -406,31 +402,29 @@
 
     mine = pl.pallas_call(
         functools.partial(kernel, n_ctx, norm),
-        out_shape=shapes,
+        out_shape=[pltpu.VMEM(t.shape, t.dtype) for t in shapes],
         in_specs=[pinned] * 7,
-        out_specs=(hbm,) * 4,
-        scratch_shapes=[chunks(T, BF16)] * 3 + [pltpu.VMEM((taps, channels), F32)] + [pltpu.VMEM(doc_bounds.shape, jnp.int32), pltpu.VMEM((1, 1), jnp.int32), pltpu.VMEM((taps, CW), F32)]
-        + [chunks(T, BF16)] * 10 + [chunks(2 * T, F32)] * 2 + [chunks(4 * T, BF16)] + [
-            pltpu.VMEM((2, NCORE, T, 2 * CW), BF16),
-            pltpu.VMEM((2, T, 2 * CW), BF16),
-            pltpu.VMEM((2, NY, T, 2 * T), BF16),
-            pltpu.VMEM((2, 3, T, 2 * T), BF16),
-            pltpu.VMEM((2, T, 2 * T), BF16),
-            pltpu.VMEM((2, 3, taps, 2 * T), BF16),
-            pltpu.VMEM((2, NX, taps, 2 * T), BF16),
-            pltpu.VMEM((2, NY * NCORE, taps, 2 * T), BF16),
+        out_specs=[pl.BlockSpec(memory_space=pltpu.VMEM)] * 4,
+        scratch_shapes=[pltpu.VMEM(doc_bounds.shape, jnp.int32), pltpu.VMEM((1, 1), jnp.int32), pltpu.VMEM((taps, channels // 2), F32)]
+        + [chunks(T, BF16)] * 5 + [pltpu.VMEM((2, n_chunk, T, CW), BF16)] * 2 + [chunks(T, BF16)] + [chunks(2 * T, F32)] * 2 + [chunks(4 * T, BF16)] + [
+            pltpu.VMEM((half, NCORE, T, CW), BF16),
+            pltpu.VMEM((half, T, CW), BF16),
+            pltpu.VMEM((half, NY, T, T), BF16),
+            pltpu.VMEM((half, 3, T, T), BF16),
+            pltpu.VMEM((half, T, T), BF16),
+            pltpu.VMEM((half, 3, taps, T), BF16),
+            pltpu.VMEM((half, NX, taps, T), BF16),
+            pltpu.VMEM((half, NY * NCORE, taps, T), BF16),
         ] + [pltpu.VMEM((2 * T, T), BF16)] * 5 + [pltpu.VMEM((4 * T, T), BF16)] + [pltpu.VMEM((T, 4 * T), BF16)] * 3 + [
-            dma((3,)), dma((3, n_chunk)), dma((4, n_chunk)), dma((2, n_chunk)), dma((2, n_chunk)),
-            dma((3,)), dma((3,)), dma((3,)), dma((3,)), dma((4,)), dma((4,)),
-            dma((2,)), dma((2,)), dma((2, 3)), dma((2, 3)), dma((2, 3)), dma((2, 3)), dma((2, 3)), dma((2, 3)),
-            dma((2, 7)), dma((2, 7)),
-        ],
+            dma((3,)), dma((4, n_chunk)), dma((2, n_chunk)), dma((2, n_chunk)),
+            dma((3,)), dma((3,)), dma((4,)), dma((4,)), dma((half,)), dma((half,)),
+        ] + [dma((half, 3))] * 6 + [dma((half, 7))] * 2,
         compiler_params=pltpu.CompilerParams(
-            collective_id=0, has_side_effects=True, vmem_limit_bytes=62 * 1024 * 1024),
+            collective_id=0, has_side_effects=True, vmem_limit_bytes=58 * 1024 * 1024),
     )(doc_bounds, continues, filters, key_proj[0], value_proj[0], query_gate[0], grad_out[0])
     out = pl.pallas_call(
-        write_out, out_shape=shapes, in_specs=[hbm] * 4, out_specs=(pinned,) * 4, scratch_shapes=[pltpu.VMEM(t.shape, t.dtype) for t in shapes] + [dma((4, 2)), dma((4, 2))],
-        compiler_params=pltpu.CompilerParams(vmem_limit_bytes=62 * 1024 * 1024),
+        write_out, out_shape=shapes, in_specs=[pl.BlockSpec(memory_space=pltpu.VMEM)] * 4, out_specs=(pinned,) * 4,
+        scratch_shapes=[dma((4, 2))], compiler_params=pltpu.CompilerParams(vmem_limit_bytes=48 * 1024 * 1024),
     )(*mine)
     return out[0][None], out[1][None], out[2][None], out[3]
 

time: 55.8 us -> 50.2 us (0.90)
  Pallas kernels: 54.4 us -> 48.9 us
    pallas_call x2, Pallas kernels: 54.4 us -> 48.9 us  [the longest x1 47 us: shards(): pl.pallas_call(functools.partial(kernel, n_ctx, norm), out_shape=[pltpu.V...]
where the time goes in v3:
time: 50.2 us; the launch traced here: 50.1 us
  Pallas kernels  48.9 us (97%)
  between operations  1.29 us (3%)
    pallas_call x1, Pallas kernels, shards(): pl.pallas_call(functools.partial(kernel, n_ctx, norm), out_shape=[pltpu.V...  47 us
    pallas_call x1, Pallas kernels, shards(): pl.pallas_call(write_out, out_shape=shapes, in_specs=[pl.BlockSpec(memory...  1.9 us

profile of v3, /device:TPU:1, one launch (start us, length us, event | category | flops | bytes accessed | tf_op | source)
XLA Modules:
  0.0 50.1 jit_solution(118756343042664303)
XLA Ops:
  1.3 47.0 %shard_map.102 = (bf16[128,4096]{1,0:T(8,128)(2,1)S(1)}, bf16[128,4096]{1,0:T(8,128)(2,1)S(1)}, bf16[128,4096]{1,0:T(8,128)(2,1)S(1)}, f32[32,4096]{1,0:T(8,128)S(1)}) custom-call(s32[1,49]{1,0:T(1,128)} %bounds_hbm.1, s32[1,1]{1,0:T(1,128)S(6)} %copy.11.cont_hbm, f32[32,4096]{1,0:T(8,128)} %filt_hbm.1, bf16[128,4096]{1,0:T(8,128)(2,1)} %bitcast.7, ...), custom_call_target="tpu_custom_call" | custom-call | tf_op jit(solution)/shard_map/pallas_call | solution.py:403
  48.2 1.9 %shard_map.103 = (bf16[128,4096]{1,0:T(8,128)(2,1)}, bf16[128,4096]{1,0:T(8,128)(2,1)}, bf16[128,4096]{1,0:T(8,128)(2,1)}, f32[32,4096]{1,0:T(8,128)}) custom-call(bf16[128,4096]{1,0:T(8,128)(2,1)S(1)} %get-tuple-element.12.a, bf16[128,4096]{1,0:T(8,128)(2,1)S(1)} %get-tuple-element.13.b, bf16[128,4096]{1,0:T(8,128)(2,1)S(1)} %get-tuple-element.14.c, ...), custom_call_target="tpu_custom_call" | custom-call | tf_op jit(solution)/shard_map/pallas_call | solution.py:425

commit v4 on v3

--- a/solution.py
+++ b/solution.py
@@ -126,6 +126,48 @@
         grad_conv = (ob[j].astype(F32) * qb[j].astype(F32)).astype(BF16)
         gb[j] = grad_conv
         edge_out[1, j] = jnp.where(head_row, grad_conv.astype(F32), 0.0).astype(BF16)
+
+    def times(a, b):
+        return [(a[0] * b[0] - a[1] * b[1]).astype(BF16), (a[0] * b[1] + a[1] * b[0]).astype(BF16)]
+
+    def times_conj(a, b):
+        return [(a[0] * b[0] + a[1] * b[1]).astype(BF16), (a[1] * b[0] - a[0] * b[1]).astype(BF16)]
+
+    def halves(a):
+        return [a[0:T], a[T:2 * T]]
+
+    def put(ref, j, start, cols, parts):
+        for i, part in enumerate(parts):
+            ref[j, pl.ds(start + i * T, T), cols] = part
+
+    pl.semaphore_wait(barrier, len(peers))
+
+    wide_rows = wb.at[own_half, own_rows, :]
+    stage1 = [send(wide_rows, wide_rows, ws1.at[d - 1], wr1.at[d - 1], {"fsdp": f_of(d)}) for d in (1, 2, 3)]
+    stage2 = [send(wide_rows, wide_rows, ws2.at[0], wr2.at[0], mate)]
+    for copy in stage1 + stage2:
+        copy.start()
+
+    def edge(way, j):
+        return send(edge_out.at[way, j], edge_in.at[way, j], hs_sem.at[way, j], hr_sem.at[way, j],
+                    {"ctx": lax.rem(ctx + 1 - 2 * way + n_ctx, n_ctx)})
+
+    def early(way, i):
+        return edge(way, way * half + i)
+
+    def late(way, i):
+        return edge(way, (1 - way) * half + i)
+
+    def depart_halo(part):
+        for way in (1 - core, core):
+            @pl.loop(0, half)
+            def _(i):
+                part(way, i).start()
+
+    depart_halo(early)
+
+
+    depart_halo(late)
 
     low = jnp.max(jnp.where(bounds <= row + first, bounds, 0.0), axis=1, keepdims=True)
     high = jnp.min(jnp.where(bounds > row + first, bounds, BIG), axis=1, keepdims=True)
@@ -169,19 +211,6 @@
         grad_m[:, cols] = jnp.where(row >= last_start, part / T, 0.0).astype(BF16)
         filt_m[:, cols] = (part * (norm / T)).astype(BF16)
 
-    def times(a, b):
-        return [(a[0] * b[0] - a[1] * b[1]).astype(BF16), (a[0] * b[1] + a[1] * b[0]).astype(BF16)]
-
-    def times_conj(a, b):
-        return [(a[0] * b[0] + a[1] * b[1]).astype(BF16), (a[1] * b[0] - a[0] * b[1]).astype(BF16)]
-
-    def halves(a):
-        return [a[0:T], a[T:2 * T]]
-
-    def put(ref, j, start, cols, parts):
-        for i, part in enumerate(parts):
-            ref[j, pl.ds(start + i * T, T), cols] = part
-
     blocks = [pl.ds(c, 256) for c in range(0, CW, 256)]
 
     @pl.loop(0, n_chunk)
@@ -192,31 +221,6 @@
             xi_s[j, :, cols] = x_in
             gi_s[j, :, cols] = g_in
             put(filt_f, j, 0, cols, times_conj(halves(g_in), halves(x_in)))
-
-    pl.semaphore_wait(barrier, len(peers))
-
-    wide_rows = wb.at[own_half, own_rows, :]
-    stage1 = [send(wide_rows, wide_rows, ws1.at[d - 1], wr1.at[d - 1], {"fsdp": f_of(d)}) for d in (1, 2, 3)]
-    stage2 = [send(wide_rows, wide_rows, ws2.at[0], wr2.at[0], mate)]
-    for copy in stage1 + stage2:
-        copy.start()
-
-    def edge(way, j):
-        return send(edge_out.at[way, j], edge_in.at[way, j], hs_sem.at[way, j], hr_sem.at[way, j],
-                    {"ctx": lax.rem(ctx + 1 - 2 * way + n_ctx, n_ctx)})
-
-    def early(way, i):
-        return edge(way, way * half + i)
-
-    def late(way, i):
-        return edge(way, (1 - way) * half + i)
-
-    for part in (early, late):
-        for way in (1 - core, core):
-            @pl.loop(0, half)
-            def _(i):
-                part(way, i).start()
-
 
     def share_filters():
         for d in (1, 2, 3):
@@ -321,15 +325,15 @@
 
     wave_work(0)
     reduce0(0)
+    reduce1(0)
     wave_work(1)
     reduce0(1)
-    reduce1(0)
+    reduce1(1)
     wave_work(2)
     reduce0(2)
-    reduce1(1)
+    reduce1(2)
     wave_work(3)
     reduce0(3)
-    reduce1(2)
     reduce1(3)
     reduce2(0)
     reduce2(1)

time: 50.2 us -> 48.5 us (0.966)
  Pallas kernels: 48.9 us -> 47.1 us
    pallas_call x1, Pallas kernels: 47 us -> 45.2 us  [shards(): pl.pallas_call(functools.partial(kernel, n_ctx, norm), out_shape=[pltpu.V...]
where the time goes in v4:
time: 48.5 us; the launch traced here: 48.4 us
  Pallas kernels  47.1 us (97%)
  between operations  1.29 us (3%)
    pallas_call x1, Pallas kernels, shards(): pl.pallas_call(functools.partial(kernel, n_ctx, norm), out_shape=[pltpu.V...  45.2 us
    pallas_call x1, Pallas kernels, shards(): pl.pallas_call(write_out, out_shape=shapes, in_specs=[pl.BlockSpec(memory...  1.9 us

profile of v4, /device:TPU:1, one launch (start us, length us, event | category | flops | bytes accessed | tf_op | source)
XLA Modules:
  0.0 48.4 jit_solution(8068349225511455503)
XLA Ops:
  1.3 45.2 %shard_map.102 = (bf16[128,4096]{1,0:T(8,128)(2,1)S(1)}, bf16[128,4096]{1,0:T(8,128)(2,1)S(1)}, bf16[128,4096]{1,0:T(8,128)(2,1)S(1)}, f32[32,4096]{1,0:T(8,128)S(1)}) custom-call(s32[1,49]{1,0:T(1,128)} %bounds_hbm.1, s32[1,1]{1,0:T(1,128)S(6)} %copy.11.cont_hbm, f32[32,4096]{1,0:T(8,128)} %filt_hbm.1, bf16[128,4096]{1,0:T(8,128)(2,1)} %bitcast.7, ...), custom_call_target="tpu_custom_call" | custom-call | tf_op jit(solution)/shard_map/pallas_call | solution.py:407
  46.5 1.9 %shard_map.103 = (bf16[128,4096]{1,0:T(8,128)(2,1)}, bf16[128,4096]{1,0:T(8,128)(2,1)}, bf16[128,4096]{1,0:T(8,128)(2,1)}, f32[32,4096]{1,0:T(8,128)}) custom-call(bf16[128,4096]{1,0:T(8,128)(2,1)S(1)} %get-tuple-element.12.a, bf16[128,4096]{1,0:T(8,128)(2,1)S(1)} %get-tuple-element.13.b, bf16[128,4096]{1,0:T(8,128)(2,1)S(1)} %get-tuple-element.14.c, ...), custom_call_target="tpu_custom_call" | custom-call | tf_op jit(solution)/shard_map/pallas_call | solution.py:429

commit v5 on v4

--- a/solution.py
+++ b/solution.py
@@ -348,18 +348,19 @@
         late(0, i).wait_recv()
         late(1, i).wait_recv()
 
-    conv_and_grad(0, 2)
+    conv_and_grad(0, 1)
     reduce3(0)
     reduce3(1)
-    conv_and_grad(2, 4)
+    conv_and_grad(1, 2)
     reduce3(2)
     reduce3(3)
+    conv_and_grad(2, 4)
     reduce4(0)
     reduce4(1)
-    conv_and_grad(4, 6)
+    conv_and_grad(4, 5)
     reduce4(2)
     reduce4(3)
-    conv_and_grad(6, 8)
+    conv_and_grad(5, n_chunk)
     reduce5(0)
     reduce5(1)
     reduce5(2)

time: 48.5 us -> 48 us (0.990)
  Pallas kernels: 47.1 us -> 46.6 us
where the time goes in v5:
time: 48 us; the launch traced here: 47.9 us
  Pallas kernels  46.6 us (97%)
  between operations  1.29 us (3%)
    pallas_call x1, Pallas kernels, shards(): pl.pallas_call(functools.partial(kernel, n_ctx, norm), out_shape=[pltpu.V...  44.7 us
    pallas_call x1, Pallas kernels, shards(): pl.pallas_call(write_out, out_shape=shapes, in_specs=[pl.BlockSpec(memory...  1.9 us

profile of v5, /device:TPU:1, one launch (start us, length us, event | category | flops | bytes accessed | tf_op | source)
XLA Modules:
  0.0 47.9 jit_solution(3259541899265315137)
XLA Ops:
  1.3 44.7 %shard_map.102 = (bf16[128,4096]{1,0:T(8,128)(2,1)S(1)}, bf16[128,4096]{1,0:T(8,128)(2,1)S(1)}, bf16[128,4096]{1,0:T(8,128)(2,1)S(1)}, f32[32,4096]{1,0:T(8,128)S(1)}) custom-call(s32[1,49]{1,0:T(1,128)} %bounds_hbm.1, s32[1,1]{1,0:T(1,128)S(6)} %copy.11.cont_hbm, f32[32,4096]{1,0:T(8,128)} %filt_hbm.1, bf16[128,4096]{1,0:T(8,128)(2,1)} %bitcast.7, ...), custom_call_target="tpu_custom_call" | custom-call | tf_op jit(solution)/shard_map/pallas_call | solution.py:408
  46.0 1.9 %shard_map.103 = (bf16[128,4096]{1,0:T(8,128)(2,1)}, bf16[128,4096]{1,0:T(8,128)(2,1)}, bf16[128,4096]{1,0:T(8,128)(2,1)}, f32[32,4096]{1,0:T(8,128)}) custom-call(bf16[128,4096]{1,0:T(8,128)(2,1)S(1)} %get-tuple-element.12.a, bf16[128,4096]{1,0:T(8,128)(2,1)S(1)} %get-tuple-element.13.b, bf16[128,4096]{1,0:T(8,128)(2,1)S(1)} %get-tuple-element.14.c, ...), custom_call_target="tpu_custom_call" | custom-call | tf_op jit(solution)/shard_map/pallas_call | solution.py:430
